TPU v7x, 128 devices: a whole 4x4x4 slice. The times are simulated.
128 devices in a mesh: dp: 8 (over z_lo, y), tensor: 16 (over x, z_hi, core).
Axes of the slice: x: 4, y: 4, z: 4 (z_hi: 2, z_lo: 2; z = z_hi * 2 + z_lo), core: 2. Of those that a mesh axis runs over, the one named last changes fastest.
Arguments:
- hidden: bfloat16 [1024, 8192], P('dp', 'tensor')
- norm_gain: float32 [8192], P('tensor'), may hold values from 0.5 to 1.5
- head: bfloat16 [8192, 147456], P(None, ('dp', 'tensor'))
- targets: int32 [1024], P('dp'), may hold values from 0 to 147455
- old_logprob: float32 [1024], P('dp'), may hold values from -20 to -1
- lengths: int32 [8], P('dp'), may hold values from 1 to 128, as said below
Outputs:
- new_logprob: float32 [1024], P('dp')
- log_ratio: float32 [1024], P('dp')
Inputs may be any that keep to these rules, and one draw needn't show every extreme that they name: `lengths`: every length is at least 1 and at most 128; some sequence has 128 live tokens and some has 1.
All inputs are finite; a program needn't handle non-finite values.
Results may differ from a plain program's by a relative error of at most 0.00094.
Values may be sent and summed in bfloat16 or wider, within the bound.
A program may use at most 128 MiB of HBM per device.

v0:
```python
import jax
import jax.numpy as jnp
from jax import lax
from jax.sharding import PartitionSpec as P

D = 8192


def joined(part, axis, combine):
    gathered = jax.tree.map(lambda a: lax.all_gather(a, axis), part)

    def take(source):
        return jax.tree.map(lambda a: lax.dynamic_index_in_dim(a, source, 0, False), gathered)

    return lax.fori_loop(
        1, lax.axis_size(axis), lambda source, state: combine(state, take(source)), take(0)
    )


def combine_stats(first, second):
    top = jnp.maximum(first[0], second[0])
    total = first[1] * jnp.exp(first[0] - top) + second[1] * jnp.exp(second[0] - top)
    return (top, total, first[2] + second[2])


def body(hidden, norm_gain, head, targets, old_logprob, lengths):
    tok_rows = hidden.shape[0]
    values = hidden.astype(jnp.float32)
    sum_sq = lax.psum(jnp.sum(values * values, axis=1), "tensor")
    scaled = lax.rsqrt(sum_sq / D + 1e-06)
    normed = (values * scaled[:, None] * norm_gain[None, :]).astype(jnp.bfloat16)
    vocab_cols = head.shape[1]
    rows, target_all = (
        lax.all_gather(normed, "dp", axis=0, tiled=True),
        lax.all_gather(targets, "dp", axis=0, tiled=True),
    )
    logits = jnp.dot(
        lax.all_gather(rows, "tensor", axis=1, tiled=True), head, preferred_element_type=jnp.float32
    )
    vocab_start = lax.axis_index(("dp", "tensor")) * vocab_cols
    block_top = jnp.max(logits, axis=1)
    block_total = jnp.sum(jnp.exp(logits - block_top[:, None]), axis=1)
    column = vocab_start + jnp.arange(vocab_cols, dtype=jnp.int32)
    hits = column[None, :] == target_all[:, None]
    block_pick = jnp.sum(jnp.where(hits, logits, jnp.float32(0.0)), axis=1)
    top, total, picked = joined(
        (block_top, block_total, block_pick), ("dp", "tensor"), combine_stats
    )
    offset = lax.axis_index("dp") * tok_rows
    top = lax.dynamic_slice_in_dim(top, offset, tok_rows, 0)
    total = lax.dynamic_slice_in_dim(total, offset, tok_rows, 0)
    picked = lax.dynamic_slice_in_dim(picked, offset, tok_rows, 0)
    seq_count = lengths.shape[0]
    position = jnp.arange(tok_rows // seq_count, dtype=jnp.int32)
    live = (position[None, :] < lengths[:, None]).reshape(-1).astype(jnp.float32)
    logprob = picked - top - jnp.log(total)
    return (live * logprob, live * (logprob - old_logprob))


def solution(mesh):
    in_specs = (
        P("dp", "tensor"),
        P("tensor"),
        P(None, ("dp", "tensor")),
        P("dp"),
        P("dp"),
        P("dp"),
    )
    out_specs = (P("dp"), P("dp"))
    return jax.shard_map(body, mesh=mesh, in_specs=in_specs, out_specs=out_specs, check_vma=False)
```

profile of v0, /device:TPU:1, one launch (start us, length us, event | category | flops | bytes accessed | tf_op | source)
XLA Modules:
  0.0 784.8 jit_solution(4431477133934320301)
XLA Ops:
  7.2 0.0 all-gather.7.cloned.1.call-start
  7.2 1.0 fusion
  8.2 34.8 %psum.7 = f32[128]{0:T(128)S(1)} all-reduce(f32[128]{0:T(128)S(1)} %fusion), channel_id=1, replica_groups=mesh['dp'=8,'tensor'=16] {'tensor'}, use_global_device_ids=true, to_apply=%region_1.0 | all-reduce | flops 128 | bytes 1024 | tf_op jit(solution)/shard_map/psum | solution.py:29
  43.1 1.6 fusion.2
  44.7 0.0 all-gather.7.cloned.1.call-update
  44.8 0.0 all-gather.9.cloned.1.call-start
  44.8 35.7 %all-gather.7.cloned.1.call-done = bf16[1024,512]{1,0:T(8,128)(2,1)} async-done(((bf16[128,512]{1,0:T(8,128)(2,1)}), bf16[1024,512]{1,0:T(8,128)(2,1)}) %all-gather.7.cloned.1.call-update) | async-done | bytes 1048592 | tf_op jit(solution)/shard_map/all_gather | solution.py:34
  80.5 0.0 all-gather.9.cloned.1.call-update
  81.2 12.9 %all-gather.3 = s32[8,1,128]{2,1,0:T(1,128)S(1)} all-gather(s32[1,1,128]{2,1,0:T(1,128)} %bitcast.20), channel_id=1, replica_groups=mesh['dp'=8,'tensor'=16] {'dp'}, dimensions={0}, use_global_device_ids=true | all-gather | bytes 4608 | tf_op jit(solution)/shard_map/all_gather | solution.py:35
  94.1 116.4 %all-gather.9.cloned.1.call-done = bf16[1024,8192]{1,0:T(8,128)(2,1)} async-done(((bf16[1024,512]{1,0:T(8,128)(2,1)}), bf16[1024,8192]{1,0:T(8,128)(2,1)}) %all-gather.9.cloned.1.call-update) | async-done | bytes 16777232 | tf_op jit(solution)/shard_map/all_gather | solution.py:38
  210.5 28.4 %fusion.3 = (f32[1024]{0:T(1024)S(1)}, f32[1024,1152]{1,0:T(8,128)}) fusion(bf16[1024,8192]{1,0:T(8,128)(2,1)} %all-gather.9.cloned.1.call-done, bf16[8192,1152]{1,0:T(8,128)(2,1)} %param.10), kind=kOutput, calls=%fused_computation.16 | convolution fusion | flops 19328532480 | bytes 40374272 | tf_op jit(solution)/shard_map/dot_general | solution.py:37
  238.8 175.9 %all-gather = f32[131072]{0:T(1024)S(1)} all-gather(f32[1024]{0:T(1024)S(1)} %get-tuple-element.205), channel_id=2, replica_groups=mesh['dp'=8,'tensor'=16] {'dp','tensor'}, dimensions={0}, use_global_device_ids=true | all-gather | bytes 528384 | tf_op jit(solution)/shard_map/all_gather | solution.py:10
  414.8 0.0 copy-start
  414.8 0.1 reshape.19
  414.9 3.2 select_reduce_fusion
  418.1 171.9 %all-gather.1 = f32[131072]{0:T(1024)S(1)} all-gather(f32[1024]{0:T(1024)S(1)} %get-tuple-element.184), channel_id=3, replica_groups=mesh['dp'=8,'tensor'=16] {'dp','tensor'}, dimensions={0}, use_global_device_ids=true | all-gather | bytes 528384 | tf_op jit(solution)/shard_map/all_gather | solution.py:10
  590.0 0.1 reshape.20
  590.1 174.7 %all-gather.2 = f32[131072]{0:T(1024)S(1)} all-gather(f32[1024]{0:T(1024)S(1)} %get-tuple-element.183), channel_id=4, replica_groups=mesh['dp'=8,'tensor'=16] {'dp','tensor'}, dimensions={0}, use_global_device_ids=true | all-gather | bytes 528384 | tf_op jit(solution)/shard_map/all_gather | solution.py:10
  764.8 0.1 reshape.21
  764.9 11.9 %while.19 = (s32[]{:T(128)}, f32[1024]{0:T(1024)S(1)}, f32[1024]{0:T(1024)S(1)}, f32[1024]{0:T(1024)S(1)}, f32[128,1024]{1,0:T(8,128)S(1)}, /*index=5*/f32[128,1...) while((s32[]{:T(128)}, f32[1024]{0:T(1024)S(1)}, f32[1024]{0:T(1024)S(1)}, ...), condition=%wide.region_6.7_spmd, body=%wide.region_5.6_spmd.sunk | while | flops 7173 | bytes 61591 | solution.py:15
  776.8 0.0 copy-done
  776.8 0.6 compare_select_fusion
  777.4 0.5 compare_select_fusion.1
  (513 shorter events, 5.7 us)
Async XLA Ops:
  7.2 73.4 %all-gather.7.cloned.1.call-start = ((), (), s32[]{:S(2)}) async-start(), calls=%async_computation | async-start | bytes 1179648 | tf_op jit(solution)/shard_map/all_gather | solution.py:34
  44.8 165.7 %all-gather.9.cloned.1.call-start = ((), (), s32[]{:S(2)}) async-start(), calls=%async_computation.1 | async-start | bytes 17825792 | tf_op jit(solution)/shard_map/all_gather | solution.py:38
  414.8 362.1 %copy-start = (f32[128]{0:T(128)S(1)}, f32[128]{0:T(128)}, u32[]{:S(2)}) copy-start(f32[128]{0:T(128)} %param.12) | copy-start | bytes 1540
Sparse Core Ops, SparseCore 0:
  44.9 35.6 all-gather.6
  82.8 127.6 all-gather.8
where the time goes:
time: 785 us
  blocking collectives  570 us (73%)
  waiting for transfers between devices  152 us (19%)
  matrix products  28.4 us (4%)
  between operations  14.7 us (2%)
  other arithmetic  9.11 us (1%)
    all_gather x3, blocking collectives, joined(): gathered = jax.tree.map(lambda a: lax.all_gather(a, axis), part)  523 us
    all_gather x1, waiting for transfers between devices, body(): lax.all_gather(rows, 'tensor', axis=1, tiled=True)  116 us
    all_gather x1, waiting for transfers between devices, body(): lax.all_gather(normed, 'dp', axis=0, tiled=True)  35.7 us
    psum x1, blocking collectives, body(): sum_sq = lax.psum(jnp.sum(values * values, axis=1), 'tensor')  34.8 us
    dot_general x1, matrix products, body(): jnp.dot(lax.all_gather(rows, 'tensor', axis=1, tiled=True), head, preferr...  28.4 us
  transfers between devices with their start and end apart: 2, of which 2 were waited for; matrix products, arithmetic and copies ran while one was open for 0% of the time, Pallas kernels for 0%

commit v1 on v0

v1 whole, which is shorter than its diff:
```python
import functools

import jax
import jax.numpy as jnp
from jax import lax
from jax.experimental import pallas as pl
from jax.experimental.pallas import tpu as pltpu
from jax.sharding import PartitionSpec as P

MESH = pl.DeviceIdType.MESH


def _barrier(nd, nt, d, t):
    barrier = pltpu.get_barrier_semaphore()
    for k in range(1, nd):
        pl.semaphore_signal(barrier, inc=1, device_id=(lax.rem(d + k, nd), t), device_id_type=MESH)
    for k in range(1, nt):
        pl.semaphore_signal(barrier, inc=1, device_id=(d, lax.rem(t + k, nt)), device_id_type=MESH)
    pl.semaphore_wait(barrier, nd - 1 + nt - 1)


def _pre_kernel(nd, nt, ssq_ref, tgt_ref, q_out, t_out, q_buf, t_buf, q_send, q_recv, t_send, t_recv, local):
    d = lax.axis_index("dp")
    t = lax.axis_index("tensor")
    _barrier(nd, nt, d, t)
    own_q = pltpu.make_async_copy(ssq_ref, q_buf.at[t], local.at[0])
    own_t = pltpu.make_async_copy(tgt_ref, t_buf.at[d], local.at[1])
    own_q.start()
    own_t.start()
    sends = []
    for k in range(1, nt):
        c = pltpu.make_async_remote_copy(
            src_ref=ssq_ref, dst_ref=q_buf.at[t], send_sem=q_send.at[k], recv_sem=q_recv.at[t],
            device_id=(d, lax.rem(t + k, nt)), device_id_type=MESH)
        c.start()
        sends.append(c)
    for k in range(1, nd):
        c = pltpu.make_async_remote_copy(
            src_ref=tgt_ref, dst_ref=t_buf.at[d], send_sem=t_send.at[k], recv_sem=t_recv.at[d],
            device_id=(lax.rem(d + k, nd), t), device_id_type=MESH)
        c.start()
        sends.append(c)
    for k in range(1, nt):
        src = lax.rem(t + nt - k, nt)
        pltpu.make_async_remote_copy(
            src_ref=ssq_ref, dst_ref=q_buf.at[src], send_sem=q_send.at[k], recv_sem=q_recv.at[src],
            device_id=(d, src), device_id_type=MESH).wait_recv()
    for k in range(1, nd):
        src = lax.rem(d + nd - k, nd)
        pltpu.make_async_remote_copy(
            src_ref=tgt_ref, dst_ref=t_buf.at[src], send_sem=t_send.at[k], recv_sem=t_recv.at[src],
            device_id=(src, t), device_id_type=MESH).wait_recv()
    for c in sends:
        c.wait_send()
    own_q.wait()
    own_t.wait()
    q_out[...] = q_buf[...]
    t_out[...] = t_buf[...]


def _stats_kernel(nd, nt, s_ref, out_ref, r1, r2, s1_send, s1_recv, s2_send, s2_recv, local):
    d = lax.axis_index("dp")
    t = lax.axis_index("tensor")
    _barrier(nd, nt, d, t)
    own1 = pltpu.make_async_copy(s_ref.at[d], r1.at[d], local.at[0])
    own1.start()
    sends = []
    for k in range(1, nd):
        peer = lax.rem(d + k, nd)
        c = pltpu.make_async_remote_copy(
            src_ref=s_ref.at[peer], dst_ref=r1.at[d], send_sem=s1_send.at[k], recv_sem=s1_recv.at[d],
            device_id=(peer, t), device_id_type=MESH)
        c.start()
        sends.append(c)
    for k in range(1, nd):
        src = lax.rem(d + nd - k, nd)
        pltpu.make_async_remote_copy(
            src_ref=s_ref.at[0], dst_ref=r1.at[src], send_sem=s1_send.at[k], recv_sem=s1_recv.at[src],
            device_id=(src, t), device_id_type=MESH).wait_recv()
    own1.wait()
    own2 = pltpu.make_async_copy(r1, r2.at[t], local.at[1])
    own2.start()
    for k in range(1, nt):
        c = pltpu.make_async_remote_copy(
            src_ref=r1, dst_ref=r2.at[t], send_sem=s2_send.at[k], recv_sem=s2_recv.at[t],
            device_id=(d, lax.rem(t + k, nt)), device_id_type=MESH)
        c.start()
        sends.append(c)
    for k in range(1, nt):
        src = lax.rem(t + nt - k, nt)
        pltpu.make_async_remote_copy(
            src_ref=r1, dst_ref=r2.at[src], send_sem=s2_send.at[k], recv_sem=s2_recv.at[src],
            device_id=(d, src), device_id_type=MESH).wait_recv()
    for c in sends:
        c.wait_send()
    own2.wait()
    out_ref[...] = r2[...]


def _vmem_call(kernel, out_shape, scratch, cid):
    n_out = len(out_shape) if isinstance(out_shape, (tuple, list)) else 1
    out_specs = [pl.BlockSpec(memory_space=pltpu.VMEM)] * n_out
    return pl.pallas_call(
        kernel,
        out_shape=out_shape,
        out_specs=out_specs if n_out > 1 else out_specs[0],
        scratch_shapes=scratch,
        compiler_params=pltpu.CompilerParams(collective_id=cid, has_side_effects=True),
    )


def _body(nd, nt, hidden, norm_gain, head, targets, old_logprob, lengths):
    tok_rows = hidden.shape[0]
    width = hidden.shape[1] * nt
    lanes = 128
    values = hidden.astype(jnp.float32)
    part_sq = jnp.sum(values * values, axis=1)

    ssq_in = jnp.zeros((8, tok_rows), jnp.float32).at[0].set(part_sq)
    tgt_in = jnp.zeros((8, tok_rows), jnp.int32).at[0].set(targets)
    pre = _vmem_call(
        functools.partial(_pre_kernel, nd, nt),
        (jax.ShapeDtypeStruct((nt, 8, tok_rows), jnp.float32),
         jax.ShapeDtypeStruct((nd, 8, tok_rows), jnp.int32)),
        [pltpu.VMEM((nt, 8, tok_rows), jnp.float32),
         pltpu.VMEM((nd, 8, tok_rows), jnp.int32),
         pltpu.SemaphoreType.DMA((nt,)), pltpu.SemaphoreType.DMA((nt,)),
         pltpu.SemaphoreType.DMA((nd,)), pltpu.SemaphoreType.DMA((nd,)),
         pltpu.SemaphoreType.DMA((2,))],
        0,
    )
    q_all, t_all = pre(ssq_in, tgt_in)
    sum_sq = jnp.sum(q_all[:, 0, :], axis=0)
    target_all = t_all[:, 0, :].reshape(nd * tok_rows)

    scaled = lax.rsqrt(sum_sq / width + 1e-06)
    normed = (values * scaled[:, None] * norm_gain[None, :]).astype(jnp.bfloat16)
    vocab_cols = head.shape[1]
    rows = lax.all_gather(normed, "dp", axis=0, tiled=True)
    logits = jnp.dot(
        lax.all_gather(rows, "tensor", axis=1, tiled=True), head, preferred_element_type=jnp.float32
    )
    vocab_start = lax.axis_index(("dp", "tensor")) * vocab_cols
    block_top = jnp.max(logits, axis=1)
    block_total = jnp.sum(jnp.exp(logits - block_top[:, None]), axis=1)
    column = vocab_start + jnp.arange(vocab_cols, dtype=jnp.int32)
    hits = column[None, :] == target_all[:, None]
    block_pick = jnp.sum(jnp.where(hits, logits, jnp.float32(0.0)), axis=1)

    stacked = jnp.stack([block_top, block_total, block_pick], axis=0).reshape(3, nd, tok_rows)
    stacked = jnp.transpose(stacked, (1, 0, 2))
    s_in = jnp.concatenate([stacked, jnp.zeros((nd, 5, tok_rows), jnp.float32)], axis=1)
    stats = _vmem_call(
        functools.partial(_stats_kernel, nd, nt),
        jax.ShapeDtypeStruct((nt, nd, 8, tok_rows), jnp.float32),
        [pltpu.VMEM((nd, 8, tok_rows), jnp.float32),
         pltpu.VMEM((nt, nd, 8, tok_rows), jnp.float32),
         pltpu.SemaphoreType.DMA((nd,)), pltpu.SemaphoreType.DMA((nd,)),
         pltpu.SemaphoreType.DMA((nt,)), pltpu.SemaphoreType.DMA((nt,)),
         pltpu.SemaphoreType.DMA((2,))],
        1,
    )(s_in)
    pieces = stats.reshape(nt * nd, 8, tok_rows)
    tops = pieces[:, 0, :]
    top = jnp.max(tops, axis=0)
    total = jnp.sum(pieces[:, 1, :] * jnp.exp(tops - top[None, :]), axis=0)
    picked = jnp.sum(pieces[:, 2, :], axis=0)

    seq_count = lengths.shape[0]
    position = jnp.arange(tok_rows // seq_count, dtype=jnp.int32)
    live = (position[None, :] < lengths[:, None]).reshape(-1).astype(jnp.float32)
    logprob = picked - top - jnp.log(total)
    return (live * logprob, live * (logprob - old_logprob))


def solution(mesh):
    nd = mesh.shape["dp"]
    nt = mesh.shape["tensor"]
    in_specs = (
        P("dp", "tensor"),
        P("tensor"),
        P(None, ("dp", "tensor")),
        P("dp"),
        P("dp"),
        P("dp"),
    )
    out_specs = (P("dp"), P("dp"))
    return jax.shard_map(
        functools.partial(_body, nd, nt), mesh=mesh, in_specs=in_specs, out_specs=out_specs, check_vma=False
    )
```

time: 785 us -> 246 us (0.31)
  blocking collectives: 570 us -> 0 us
  Pallas kernels: 0 us -> 33.5 us
  waiting for transfers between devices: 152 us -> 160 us
    all_gather x4 -> x0, blocking collectives: 535 us -> none  [the longest x3 523 us: joined(): gathered = jax.tree.map(lambda a: lax.all_gather(a, axis), part)]
    psum x1 -> x0, blocking collectives: 34.8 us -> none  [body(): sum_sq = lax.psum(jnp.sum(values * values, axis=1), 'tensor')]
    pallas_call x0 -> x2, Pallas kernels: none -> 33.5 us  [the longest x1 18.2 us: _body(): _vmem_call(functools.partial(_stats_kernel, nd, nt), jax.ShapeDtypeStruct...]
    all_gather x2, waiting for transfers between devices: 152 us -> 160 us  [the longest x1 129 us: _body(): lax.all_gather(rows, 'tensor', axis=1, tiled=True)]
where the time goes in v1:
time: 246 us
  waiting for transfers between devices  160 us (65%)
  Pallas kernels  33.5 us (14%)
  matrix products  26.4 us (11%)
  between operations  14.7 us (6%)
  other arithmetic  7.49 us (3%)
  local copies, waits for them, and re-layouts  3.23 us (1%)
    all_gather x1, waiting for transfers between devices, _body(): lax.all_gather(rows, 'tensor', axis=1, tiled=True)  129 us
    all_gather x1, waiting for transfers between devices, _body(): rows = lax.all_gather(normed, 'dp', axis=0, tiled=True)  31.7 us
    dot_general x1, matrix products, _body(): jnp.dot(lax.all_gather(rows, 'tensor', axis=1, tiled=True), head, preferr...  26.4 us
    pallas_call x1, Pallas kernels, _body(): _vmem_call(functools.partial(_stats_kernel, nd, nt), jax.ShapeDtypeStruct...  18.2 us
    pallas_call x1, Pallas kernels, _body(): q_all, t_all = pre(ssq_in, tgt_in)  15.3 us
  transfers between devices with their start and end apart: 2, of which 2 were waited for; matrix products, arithmetic and copies ran while one was open for 0% of the time, Pallas kernels for 0%

profile of v1, /device:TPU:1, one launch (start us, length us, event | category | flops | bytes accessed | tf_op | source)
XLA Modules:
  0.0 245.7 jit_solution(4636082789612043227)
XLA Ops:
  7.2 0.0 all-gather.3.cloned.1.call-start
  7.2 1.0 fusion
  8.2 0.6 scatter.6.ssq_ref
  8.8 1.2 scatter.9.tgt_ref
  10.1 15.3 %shard_map.77 = (f32[16,8,128]{2,1,0:T(8,128)}, s32[8,8,128]{2,1,0:T(8,128)}) custom-call(f32[8,128]{1,0:T(8,128)} %scatter.6.ssq_ref, s32[8,128]{1,0:T(8,128)} %scatter.9.tgt_ref), custom_call_target="tpu_custom_call" | custom-call | tf_op jit(solution)/shard_map/pallas_call | solution.py:132
  25.4 0.9 slice_reduce_fusion.1
  26.3 1.6 fusion.2
  27.9 0.0 all-gather.3.cloned.1.call-update
  27.9 0.0 all-gather.5.cloned.1.call-start
  28.0 31.7 %all-gather.3.cloned.1.call-done = bf16[1024,512]{1,0:T(8,128)(2,1)} async-done(((bf16[128,512]{1,0:T(8,128)(2,1)}), bf16[1024,512]{1,0:T(8,128)(2,1)}) %all-gather.3.cloned.1.call-update) | async-done | bytes 1048592 | tf_op jit(solution)/shard_map/all_gather | solution.py:139
  59.7 0.0 all-gather.5.cloned.1.call-update
  60.4 0.8 slice.44
  61.1 128.5 %all-gather.5.cloned.1.call-done = bf16[1024,8192]{1,0:T(8,128)(2,1)} async-done(((bf16[1024,512]{1,0:T(8,128)(2,1)}), bf16[1024,8192]{1,0:T(8,128)(2,1)}) %all-gather.5.cloned.1.call-update) | async-done | bytes 16777232 | tf_op jit(solution)/shard_map/all_gather | solution.py:141
  189.6 26.4 %fusion.3 = (f32[1024]{0:T(1024)S(1)}, f32[1024,1152]{1,0:T(8,128)S(1)}) fusion(bf16[1024,8192]{1,0:T(8,128)(2,1)} %all-gather.5.cloned.1.call-done, bf16[8192,1152]{1,0:T(8,128)(2,1)} %param.12), kind=kOutput, calls=%fused_computation.16 | convolution fusion | flops 19328532480 | bytes 40374272 | tf_op jit(solution)/shard_map/dot_general | solution.py:140
  216.0 0.0 copy-start
  216.0 1.8 exponential_reduce_fusion
  217.8 0.6 concatenate.8.s_ref
  218.4 18.2 %shard_map.78 = f32[16,8,8,128]{3,2,1,0:T(8,128)} custom-call(f32[8,8,128]{2,1,0:T(8,128)} %concatenate.8.s_ref), custom_call_target="tpu_custom_call" | custom-call | tf_op jit(solution)/shard_map/pallas_call | solution.py:153
  236.6 1.6 slice_reduce_fusion
  238.3 0.0 copy-done
  238.3 0.5 compare_select_fusion
  (5 shorter events, 0.1 us)
Async XLA Ops:
  7.2 52.5 %all-gather.3.cloned.1.call-start = ((), (), s32[]{:S(2)}) async-start(), calls=%async_computation | async-start | bytes 1179648 | tf_op jit(solution)/shard_map/all_gather | solution.py:139
  27.9 161.7 %all-gather.5.cloned.1.call-start = ((), (), s32[]{:S(2)}) async-start(), calls=%async_computation.1 | async-start | bytes 17825792 | tf_op jit(solution)/shard_map/all_gather | solution.py:141
  216.0 22.3 %copy-start = (f32[128]{0:T(128)S(1)}, f32[128]{0:T(128)}, u32[]{:S(2)}) copy-start(f32[128]{0:T(128)} %param.14) | copy-start | bytes 1540
Sparse Core Ops, SparseCore 0:
  28.0 31.6 all-gather.2
  61.9 127.6 all-gather.4

commit v2 on v1

--- a/solution.py
+++ b/solution.py
@@ -95,6 +95,151 @@
         c.wait_send()
     own2.wait()
     out_ref[...] = r2[...]
+
+
+ORDERS = (("x", "y", "z"), ("y", "z", "x"), ("z", "x", "y"))
+PARTS = (48, 48, 32)
+RING = 4
+
+
+def _wrap(v):
+    return lax.rem(v + RING, RING)
+
+
+def _slab(order, k, cd):
+    full = (cd[order[2]], cd[order[1]], cd[order[0]])
+    return full[: 3 - k]
+
+
+def _gather_kernel(x_ref, o0, o1, o2, ssem, rsem, psend, precv, lsem):
+    outs = (o0, o1, o2)
+    d = lax.axis_index("dp")
+    t = lax.axis_index("tensor")
+    cc = lax.rem(t, 2)
+    me = {"x": t // 4, "y": lax.rem(d, 4), "z": (lax.rem(t // 2, 2)) * 2 + d // 4}
+
+    def dev(cd):
+        return (lax.rem(cd["z"], 2) * 4 + cd["y"], cd["x"] * 4 + (cd["z"] // 2) * 2 + cc)
+
+    def moved(dim, delta):
+        cd = dict(me)
+        cd[dim] = _wrap(me[dim] + delta)
+        return cd
+
+    partner = (d, t + 1 - 2 * cc)
+    barrier = pltpu.get_barrier_semaphore()
+    for dim in ("x", "y", "z"):
+        for delta in (1, -1):
+            pl.semaphore_signal(barrier, inc=1, device_id=dev(moved(dim, delta)), device_id_type=MESH)
+    pl.semaphore_signal(barrier, inc=1, device_id=partner, device_id_type=MESH)
+    pl.semaphore_wait(barrier, 7)
+
+    def view(r, slot, idx, k, half):
+        tail = ()
+        if half is not None:
+            tail = (slice(None),) * (k + 1) + (pl.ds(half * 256, 256),)
+        return outs[r].at[(slot,) + idx + tail]
+
+    fwd = []
+
+    def to_partner(r, j, idx, k, half):
+        c = pltpu.make_async_remote_copy(
+            src_ref=view(r, cc, idx, k, half), dst_ref=view(r, cc, idx, k, half),
+            send_sem=psend.at[r * 13 + j], recv_sem=precv.at[r * 13 + j],
+            device_id=partner, device_id_type=MESH)
+        c.start()
+        fwd.append((c, view(r, 1 - cc, idx, k, half), r * 13 + j))
+
+    own = []
+    off = 0
+    for r in range(3):
+        idx = _slab(ORDERS[r], 0, me)
+        c = pltpu.make_async_copy(x_ref.at[pl.ds(off, PARTS[r])], view(r, cc, idx, 0, None), lsem.at[r])
+        c.start()
+        own.append(c)
+        off += PARTS[r]
+    for r in range(3):
+        own[r].wait()
+        to_partner(r, 0, _slab(ORDERS[r], 0, me), 0, None)
+
+    sends = []
+    for k in range(3):
+        for r in range(3):
+            dim = ORDERS[r][k]
+            idx = _slab(ORDERS[r], k, me)
+            for di, delta in enumerate((1, -1)):
+                s = (r * 3 + k) * 4 + di
+                c = pltpu.make_async_remote_copy(
+                    src_ref=view(r, cc, idx, k, None), dst_ref=view(r, cc, idx, k, None),
+                    send_sem=ssem.at[s], recv_sem=rsem.at[s],
+                    device_id=dev(moved(dim, delta)), device_id_type=MESH)
+                c.start()
+                sends.append(c)
+        for r in range(3):
+            dim = ORDERS[r][k]
+            for di, delta in enumerate((1, -1)):
+                s = (r * 3 + k) * 4 + di
+                src_idx = _slab(ORDERS[r], k, moved(dim, -delta))
+                pltpu.make_async_remote_copy(
+                    src_ref=view(r, cc, src_idx, k, None), dst_ref=view(r, cc, src_idx, k, None),
+                    send_sem=ssem.at[s], recv_sem=rsem.at[s],
+                    device_id=dev(moved(dim, -delta)), device_id_type=MESH).wait_recv()
+                to_partner(r, 1 + 4 * k + di, src_idx, k, None)
+            for di, delta in enumerate((1, -1)):
+                s = (r * 3 + k) * 4 + 2 + di
+                src_idx = _slab(ORDERS[r], k, moved(dim, -delta))
+                c = pltpu.make_async_remote_copy(
+                    src_ref=view(r, cc, src_idx, k, di), dst_ref=view(r, cc, src_idx, k, di),
+                    send_sem=ssem.at[s], recv_sem=rsem.at[s],
+                    device_id=dev(moved(dim, delta)), device_id_type=MESH)
+                c.start()
+                sends.append(c)
+        for r in range(3):
+            dim = ORDERS[r][k]
+            for di, delta in enumerate((1, -1)):
+                s = (r * 3 + k) * 4 + 2 + di
+                far_idx = _slab(ORDERS[r], k, moved(dim, 2))
+                pltpu.make_async_remote_copy(
+                    src_ref=view(r, cc, far_idx, k, di), dst_ref=view(r, cc, far_idx, k, di),
+                    send_sem=ssem.at[s], recv_sem=rsem.at[s],
+                    device_id=dev(moved(dim, -delta)), device_id_type=MESH).wait_recv()
+                to_partner(r, 3 + 4 * k + di, far_idx, k, di)
+    for c in sends:
+        c.wait_send()
+    for c, dst, j in fwd:
+        c.wait_send()
+        pltpu.make_async_remote_copy(
+            src_ref=dst, dst_ref=dst, send_sem=psend.at[j], recv_sem=precv.at[j],
+            device_id=partner, device_id_type=MESH).wait_recv()
+
+
+def _gather(normed):
+    rows, cols = normed.shape
+    call = pl.pallas_call(
+        _gather_kernel,
+        out_shape=[jax.ShapeDtypeStruct((2, RING, RING, RING, p, cols), normed.dtype) for p in PARTS],
+        in_specs=[pl.BlockSpec(memory_space=pltpu.VMEM)],
+        out_specs=[pl.BlockSpec(memory_space=pl.ANY)] * 3,
+        scratch_shapes=[
+            pltpu.SemaphoreType.DMA((36,)), pltpu.SemaphoreType.DMA((36,)),
+            pltpu.SemaphoreType.DMA((39,)), pltpu.SemaphoreType.DMA((39,)),
+            pltpu.SemaphoreType.DMA((3,)),
+        ],
+        compiler_params=pltpu.CompilerParams(collective_id=2, has_side_effects=True),
+    )
+    bufs = call(normed)
+    parts = []
+    for r, buf in enumerate(bufs):
+        a0, a1, a2 = ORDERS[r]
+        names = ["c", a2, a1, a0, "i", "f"]
+        zpos = names.index("z")
+        shape = list(buf.shape)
+        buf = buf.reshape(shape[:zpos] + [2, 2] + shape[zpos + 1:])
+        names = names[:zpos] + ["h", "l"] + names[zpos + 1:]
+        perm = [names.index(n) for n in ("l", "y", "i", "x", "h", "c", "f")]
+        buf = jnp.transpose(buf, perm)
+        parts.append(buf.reshape(2 * RING, PARTS[r], RING * 2 * 2 * cols))
+    return jnp.concatenate(parts, axis=1).reshape(2 * RING * rows, RING * 2 * 2 * cols)
 
 
 def _vmem_call(kernel, out_shape, scratch, cid):
@@ -136,10 +281,7 @@
     scaled = lax.rsqrt(sum_sq / width + 1e-06)
     normed = (values * scaled[:, None] * norm_gain[None, :]).astype(jnp.bfloat16)
     vocab_cols = head.shape[1]
-    rows = lax.all_gather(normed, "dp", axis=0, tiled=True)
-    logits = jnp.dot(
-        lax.all_gather(rows, "tensor", axis=1, tiled=True), head, preferred_element_type=jnp.float32
-    )
+    logits = jnp.dot(_gather(normed), head, preferred_element_type=jnp.float32)
     vocab_start = lax.axis_index(("dp", "tensor")) * vocab_cols
     block_top = jnp.max(logits, axis=1)
     block_total = jnp.sum(jnp.exp(logits - block_top[:, None]), axis=1)

time: 246 us -> 204 us (0.83)
  waiting for transfers between devices: 160 us -> 0 us
  local copies, waits for them, and re-layouts: 3.23 us -> 67.3 us
  Pallas kernels: 33.5 us -> 86 us
  between operations: 14.7 us -> 1.35 us
  other arithmetic: 7.49 us -> 15.5 us
  matrix products: 26.4 us -> 32.7 us
    all_gather x2 -> x0, waiting for transfers between devices: 160 us -> none  [the longest x1 129 us: _body(): lax.all_gather(rows, 'tensor', axis=1, tiled=True)]
    reshape x0 -> x6, local copies, waits for them, and re-layouts: none -> 64.1 us  [the longest x3 34.1 us: _gather(): buf = buf.reshape(shape[:zpos] + [2, 2] + shape[zpos + 1:])]
    pallas_call x0 -> x1, Pallas kernels: none -> 53 us  [_gather(): bufs = call(normed)]
    concatenate x0 -> x1, other arithmetic: none -> 7.98 us  [_gather(): jnp.concatenate(parts, axis=1).reshape(2 * RING * rows, RING * 2 * 2 * cols)]
    dot_general x1, matrix products: 26.4 us -> 32.7 us  [_body(): logits = jnp.dot(_gather(normed), head, preferred_element_type=jnp.float32)]
  transfers between devices with their start and end apart: 2 -> 0, of which waited for: 2 -> 0; matrix products, arithmetic and copies ran while one was open for 0% -> 0% of each run, Pallas kernels for 0% -> 0%
where the time goes in v2:
time: 204 us; the launch traced here: 203 us
  Pallas kernels  86 us (42%)
  local copies, waits for them, and re-layouts  67.3 us (33%)
  matrix products  32.7 us (16%)
  other arithmetic  15.5 us (8%)
    pallas_call x1, Pallas kernels, _gather(): bufs = call(normed)  53 us
    reshape x3, local copies, waits for them, and re-layouts, _gather(): buf = buf.reshape(shape[:zpos] + [2, 2] + shape[zpos + 1:])  34.1 us
    dot_general x1, matrix products, _body(): logits = jnp.dot(_gather(normed), head, preferred_element_type=jnp.float32)  32.7 us
    reshape x3, local copies, waits for them, and re-layouts, _gather(): parts.append(buf.reshape(2 * RING, PARTS[r], RING * 2 * 2 * cols))  30 us
    pallas_call x1, Pallas kernels, _body(): _vmem_call(functools.partial(_stats_kernel, nd, nt), jax.ShapeDtypeStruct...  17.7 us
    pallas_call x1, Pallas kernels, _body(): q_all, t_all = pre(ssq_in, tgt_in)  15.3 us
    concatenate x1, other arithmetic, _gather(): jnp.concatenate(parts, axis=1).reshape(2 * RING * rows, RING * 2 * 2 * cols)  7.98 us

profile of v2, /device:TPU:1, one launch (start us, length us, event | category | flops | bytes accessed | tf_op | source)
XLA Modules:
  0.0 202.8 jit_solution(17377634069967980887)
XLA Ops:
  1.3 1.0 fusion
  2.3 0.6 scatter.6.ssq_ref
  2.9 1.2 scatter.9.tgt_ref
  4.2 15.3 %shard_map.77 = (f32[16,8,128]{2,1,0:T(8,128)}, s32[8,8,128]{2,1,0:T(8,128)}) custom-call(f32[8,128]{1,0:T(8,128)} %scatter.6.ssq_ref, s32[8,128]{1,0:T(8,128)} %scatter.9.tgt_ref), custom_call_target="tpu_custom_call" | custom-call | tf_op jit(solution)/shard_map/pallas_call | solution.py:277
  19.5 0.9 slice_reduce_fusion.1
  20.3 0.8 slice.44
  21.1 1.7 fusion.2.x_ref
  22.8 53.0 %shard_map.78 = (bf16[2,4,4,4,48,512]{5,4,3,2,1,0:T(8,128)(2,1)}, bf16[2,4,4,4,48,512]{5,4,3,2,1,0:T(8,128)(2,1)}, bf16[2,4,4,4,32,512]{5,4,3,2,1,0:T(8,128)(2,1)}) custom-call(bf16[128,512]{1,0:T(8,128)(2,1)} %fusion.2.x_ref), custom_call_target="tpu_custom_call" | custom-call | tf_op jit(solution)/shard_map/pallas_call | solution.py:230
  75.8 12.8 %copy.18 = bf16[2,2,2,4,4,48,512]{6,0,1,4,5,3,2:T(2,128)(2,1)} copy(bf16[2,2,2,4,4,48,512]{6,5,4,3,2,1,0:T(8,128)(2,1)} %bitcast.35) | data formatting | bytes 12582912 | tf_op jit(solution)/shard_map/reshape | solution.py:237
  88.6 11.1 %reshape.111 = bf16[8,48,8192]{2,1,0:T(8,128)(2,1)} reshape(bf16[2,4,48,4,2,2,512]{6,5,4,3,2,1,0:T(2,128)(2,1)} %bitcast.30) | data formatting | bytes 12582912 | tf_op jit(solution)/shard_map/reshape | solution.py:241
  99.7 12.8 %copy.17 = bf16[2,4,2,2,4,48,512]{6,0,2,1,5,4,3:T(2,128)(2,1)} copy(bf16[2,4,2,2,4,48,512]{6,5,4,3,2,1,0:T(8,128)(2,1)} %bitcast.34) | data formatting | bytes 12582912 | tf_op jit(solution)/shard_map/reshape | solution.py:237
  112.4 11.1 %reshape.113 = bf16[8,48,8192]{2,1,0:T(8,128)(2,1)} reshape(bf16[2,4,48,4,2,2,512]{6,5,4,3,2,1,0:T(2,128)(2,1)} %bitcast.31) | data formatting | bytes 12582912 | tf_op jit(solution)/shard_map/reshape | solution.py:241
  123.6 8.5 %copy.19 = bf16[2,4,4,2,2,32,512]{6,0,3,2,5,1,4:T(2,128)(2,1)} copy(bf16[2,4,4,2,2,32,512]{6,5,4,3,2,1,0:T(8,128)(2,1)} %bitcast.36) | data formatting | bytes 8388608 | tf_op jit(solution)/shard_map/reshape | solution.py:237
  132.1 7.8 %reshape.115 = bf16[8,32,8192]{2,1,0:T(8,128)(2,1)} reshape(bf16[2,4,32,4,2,2,512]{6,5,4,3,2,1,0:T(2,128)(2,1)} %bitcast.33) | data formatting | bytes 8388608 | tf_op jit(solution)/shard_map/reshape | solution.py:241
  139.9 8.0 %pad_maximum_fusion = bf16[8,128,8192]{2,1,0:T(8,128)(2,1)S(1)} fusion(bf16[8,32,8192]{2,1,0:T(8,128)(2,1)} %reshape.115, bf16[8,48,8192]{2,1,0:T(8,128)(2,1)} %reshape.113, bf16[8,48,8192]{2,1,0:T(8,128)(2,1)} %reshape.111), kind=kLoop, calls=%fused_computation | loop fusion | flops 50331648 | bytes 33554432 | tf_op jit(solution)/shard_map/concatenate | solution.py:242
  147.9 0.0 copy-start
  147.9 32.7 %fusion.3 = (f32[1024]{0:T(1024)S(1)}, f32[1024,1152]{1,0:T(8,128)S(1)}) fusion(bf16[1024,8192]{1,0:T(8,128)(2,1)S(1)} %bitcast.32, bf16[8192,1152]{1,0:T(8,128)(2,1)} %param.12), kind=kOutput, calls=%fused_computation.20 | convolution fusion | flops 19328532480 | bytes 40374272 | tf_op jit(solution)/shard_map/dot_general | solution.py:284
  180.5 1.8 exponential_reduce_fusion
  182.3 0.6 concatenate.12.s_ref
  182.9 17.7 %shard_map.79 = f32[16,8,8,128]{3,2,1,0:T(8,128)} custom-call(f32[8,8,128]{2,1,0:T(8,128)} %concatenate.12.s_ref), custom_call_target="tpu_custom_call" | custom-call | tf_op jit(solution)/shard_map/pallas_call | solution.py:295
  200.6 1.6 slice_reduce_fusion
  202.3 0.0 copy-done
  202.3 0.5 compare_select_fusion
  (5 shorter events, 0.1 us)
Async XLA Ops:
  147.9 54.4 %copy-start = (f32[128]{0:T(128)S(1)}, f32[128]{0:T(128)}, u32[]{:S(2)}) copy-start(f32[128]{0:T(128)} %param.14) | copy-start | bytes 1540

commit v3 on v1

--- a/solution.py
+++ b/solution.py
@@ -95,6 +95,145 @@
         c.wait_send()
     own2.wait()
     out_ref[...] = r2[...]
+
+
+ORDERS = (("x", "y", "z"), ("y", "z", "x"), ("z", "x", "y"))
+PARTS = (48, 48, 32)
+RING = 4
+
+
+def _wrap(v):
+    return lax.rem(v + RING, RING)
+
+
+def _gather_kernel(x_ref, out, ssem, rsem, psend, precv, lsem):
+    d = lax.axis_index("dp")
+    t = lax.axis_index("tensor")
+    cc = lax.rem(t, 2)
+    me = {"x": t // 4, "y": lax.rem(d, 4), "z": (lax.rem(t // 2, 2)) * 2 + d // 4}
+    cols = x_ref.shape[1]
+    half_cols = cols // 2
+
+    def dev(cd):
+        return (lax.rem(cd["z"], 2) * 4 + cd["y"], cd["x"] * 4 + (cd["z"] // 2) * 2 + cc)
+
+    def moved(cd, dim, delta):
+        cd = dict(cd)
+        cd[dim] = _wrap(cd[dim] + delta)
+        return cd
+
+    def slab(r, k, center):
+        found = [center]
+        for dim in ORDERS[r][:k]:
+            found = [dict(cd, **{dim: v}) for cd in found for v in range(RING)]
+        return found
+
+    offs = (0, PARTS[0], PARTS[0] + PARTS[1])
+
+    def piece(cd, core, r, half):
+        row = (lax.rem(cd["z"], 2) * 4 + cd["y"]) * x_ref.shape[0] + offs[r]
+        col = (cd["x"] * 4 + (cd["z"] // 2) * 2 + core) * cols
+        if half is None:
+            return out.at[pl.ds(pl.multiple_of(row, 16), PARTS[r]), pl.ds(pl.multiple_of(col, cols), cols)]
+        col = col + half * half_cols
+        return out.at[pl.ds(pl.multiple_of(row, 16), PARTS[r]), pl.ds(pl.multiple_of(col, half_cols), half_cols)]
+
+    partner = (d, t + 1 - 2 * cc)
+    barrier = pltpu.get_barrier_semaphore()
+    for dim in ("x", "y", "z"):
+        for delta in (1, -1):
+            pl.semaphore_signal(barrier, inc=1, device_id=dev(moved(me, dim, delta)), device_id_type=MESH)
+    pl.semaphore_signal(barrier, inc=1, device_id=partner, device_id_type=MESH)
+    pl.semaphore_wait(barrier, 7)
+
+    fwd = []
+
+    def to_partner(r, j, cds, half):
+        for cd in cds:
+            v = piece(cd, cc, r, half)
+            pltpu.make_async_remote_copy(
+                src_ref=v, dst_ref=v, send_sem=psend.at[r * 13 + j], recv_sem=precv.at[r * 13 + j],
+                device_id=partner, device_id_type=MESH).start()
+        fwd.append((r * 13 + j, len(cds), r, half))
+
+    own = []
+    off = 0
+    for r in range(3):
+        c = pltpu.make_async_copy(x_ref.at[pl.ds(off, PARTS[r])], piece(me, cc, r, None), lsem.at[r])
+        c.start()
+        own.append(c)
+        off += PARTS[r]
+    for r in range(3):
+        own[r].wait()
+        to_partner(r, 0, [me], None)
+
+    def whole(n, r, half):
+        return out.at[pl.ds(0, n * PARTS[r]), pl.ds(0, cols if half is None else half_cols)]
+
+    def recv(group, cds, r, half, src_dev):
+        v = whole(len(cds), r, half)
+        pltpu.make_async_remote_copy(
+            src_ref=v, dst_ref=v, send_sem=ssem.at[group], recv_sem=rsem.at[group],
+            device_id=src_dev, device_id_type=MESH).wait_recv()
+
+    sends = []
+
+    def send(group, cds, r, half, dst_dev):
+        for cd in cds:
+            v = piece(cd, cc, r, half)
+            pltpu.make_async_remote_copy(
+                src_ref=v, dst_ref=v, send_sem=ssem.at[group], recv_sem=rsem.at[group],
+                device_id=dst_dev, device_id_type=MESH).start()
+        v = whole(len(cds), r, half)
+        sends.append(pltpu.make_async_remote_copy(
+            src_ref=v, dst_ref=v, send_sem=ssem.at[group], recv_sem=rsem.at[group],
+            device_id=dst_dev, device_id_type=MESH))
+
+    for k in range(3):
+        for r in range(3):
+            dim = ORDERS[r][k]
+            for di, delta in enumerate((1, -1)):
+                send((r * 3 + k) * 4 + di, slab(r, k, me), r, None, dev(moved(me, dim, delta)))
+        for r in range(3):
+            dim = ORDERS[r][k]
+            for di, delta in enumerate((1, -1)):
+                near = slab(r, k, moved(me, dim, -delta))
+                recv((r * 3 + k) * 4 + di, near, r, None, dev(moved(me, dim, -delta)))
+                to_partner(r, 1 + 4 * k + di, near, None)
+            for di, delta in enumerate((1, -1)):
+                near = slab(r, k, moved(me, dim, -delta))
+                send((r * 3 + k) * 4 + 2 + di, near, r, di, dev(moved(me, dim, delta)))
+        for r in range(3):
+            dim = ORDERS[r][k]
+            far = slab(r, k, moved(me, dim, 2))
+            for di, delta in enumerate((1, -1)):
+                recv((r * 3 + k) * 4 + 2 + di, far, r, di, dev(moved(me, dim, -delta)))
+                to_partner(r, 3 + 4 * k + di, far, di)
+    for c in sends:
+        c.wait_send()
+    for j, n, r, half in fwd:
+        v = whole(n, r, half)
+        c = pltpu.make_async_remote_copy(
+            src_ref=v, dst_ref=v, send_sem=psend.at[j], recv_sem=precv.at[j],
+            device_id=partner, device_id_type=MESH)
+        c.wait_send()
+        c.wait_recv()
+
+
+def _gather(normed):
+    rows, cols = normed.shape
+    return pl.pallas_call(
+        _gather_kernel,
+        out_shape=jax.ShapeDtypeStruct((2 * RING * rows, RING * 2 * 2 * cols), normed.dtype),
+        in_specs=[pl.BlockSpec(memory_space=pltpu.VMEM)],
+        out_specs=pl.BlockSpec(memory_space=pl.ANY),
+        scratch_shapes=[
+            pltpu.SemaphoreType.DMA((36,)), pltpu.SemaphoreType.DMA((36,)),
+            pltpu.SemaphoreType.DMA((39,)), pltpu.SemaphoreType.DMA((39,)),
+            pltpu.SemaphoreType.DMA((3,)),
+        ],
+        compiler_params=pltpu.CompilerParams(collective_id=2, has_side_effects=True),
+    )(normed)
 
 
 def _vmem_call(kernel, out_shape, scratch, cid):
@@ -136,10 +275,7 @@
     scaled = lax.rsqrt(sum_sq / width + 1e-06)
     normed = (values * scaled[:, None] * norm_gain[None, :]).astype(jnp.bfloat16)
     vocab_cols = head.shape[1]
-    rows = lax.all_gather(normed, "dp", axis=0, tiled=True)
-    logits = jnp.dot(
-        lax.all_gather(rows, "tensor", axis=1, tiled=True), head, preferred_element_type=jnp.float32
-    )
+    logits = jnp.dot(_gather(normed), head, preferred_element_type=jnp.float32)
     vocab_start = lax.axis_index(("dp", "tensor")) * vocab_cols
     block_top = jnp.max(logits, axis=1)
     block_total = jnp.sum(jnp.exp(logits - block_top[:, None]), axis=1)

time: 246 us -> 125 us (0.51)
  waiting for transfers between devices: 160 us -> 0 us
  Pallas kernels: 33.5 us -> 86.5 us
  between operations: 14.7 us -> 1.34 us
    all_gather x2 -> x0, waiting for transfers between devices: 160 us -> none  [the longest x1 129 us: _body(): lax.all_gather(rows, 'tensor', axis=1, tiled=True)]
    pallas_call x0 -> x1, Pallas kernels: none -> 53.3 us  [_gather(): pl.pallas_call(_gather_kernel, out_shape=jax.ShapeDtypeStruct((2 * RING *...]
  transfers between devices with their start and end apart: 2 -> 0, of which waited for: 2 -> 0; matrix products, arithmetic and copies ran while one was open for 0% -> 0% of each run, Pallas kernels for 0% -> 0%
where the time goes in v3:
time: 125 us
  Pallas kernels  86.5 us (69%)
  matrix products  26.4 us (21%)
  other arithmetic  7.48 us (6%)
  local copies, waits for them, and re-layouts  3.24 us (3%)
  between operations  1.34 us (1%)
    pallas_call x1, Pallas kernels, _gather(): pl.pallas_call(_gather_kernel, out_shape=jax.ShapeDtypeStruct((2 * RING *...  53.3 us
    dot_general x1, matrix products, _body(): logits = jnp.dot(_gather(normed), head, preferred_element_type=jnp.float32)  26.4 us
    pallas_call x1, Pallas kernels, _body(): _vmem_call(functools.partial(_stats_kernel, nd, nt), jax.ShapeDtypeStruct...  17.9 us
    pallas_call x1, Pallas kernels, _body(): q_all, t_all = pre(ssq_in, tgt_in)  15.3 us

profile of v3, /device:TPU:1, one launch (start us, length us, event | category | flops | bytes accessed | tf_op | source)
XLA Modules:
  0.0 124.9 jit_solution(15296788870532984933)
XLA Ops:
  1.3 1.0 fusion
  2.3 0.6 scatter.6.ssq_ref
  2.9 1.3 %scatter.9.tgt_ref = s32[8,128]{1,0:T(8,128)} pad(s32[1,128]{1,0:T(1,128)} %bitcast.26, s32[]{:T(128)} %constant.64.clone.1), padding=0_7x0_0 | pad | bytes 4612 | tf_op jit(solution)/shard_map/scatter | solution.py:259
  4.2 15.3 %shard_map.77 = (f32[16,8,128]{2,1,0:T(8,128)}, s32[8,8,128]{2,1,0:T(8,128)}) custom-call(f32[8,128]{1,0:T(8,128)} %scatter.6.ssq_ref, s32[8,128]{1,0:T(8,128)} %scatter.9.tgt_ref), custom_call_target="tpu_custom_call" | custom-call | tf_op jit(solution)/shard_map/pallas_call | solution.py:271
  19.5 0.9 slice_reduce_fusion.1
  20.3 0.8 slice.44
  21.1 1.6 %fusion.2.x_ref = bf16[128,512]{1,0:T(8,128)(2,1)} fusion(bf16[128,512]{1,0:T(8,128)(2,1)} %param.10, f32[512]{0:T(512)} %param.11, f32[128]{0:T(128)S(1)} %add_rsqrt_fusion), kind=kLoop, calls=%fused_computation.6 | loop fusion | flops 262144 | bytes 264704 | tf_op jit(solution)/shard_map/convert_element_type | solution.py:276
  22.7 53.3 %shard_map.78 = bf16[1024,8192]{1,0:T(8,128)(2,1)} custom-call(bf16[128,512]{1,0:T(8,128)(2,1)} %fusion.2.x_ref), custom_call_target="tpu_custom_call" | custom-call | tf_op jit(solution)/shard_map/pallas_call | solution.py:225
  76.1 26.4 %fusion.3 = (f32[1024]{0:T(1024)S(1)}, f32[1024,1152]{1,0:T(8,128)S(1)}) fusion(bf16[1024,8192]{1,0:T(8,128)(2,1)} %shard_map.78, bf16[8192,1152]{1,0:T(8,128)(2,1)} %param.12), kind=kOutput, calls=%fused_computation.16 | convolution fusion | flops 19328532480 | bytes 40374272 | tf_op jit(solution)/shard_map/dot_general | solution.py:278
  102.4 0.0 copy-start
  102.5 1.8 %exponential_reduce_fusion = (f32[1024]{0:T(1024)S(1)}, f32[1024]{0:T(1024)S(1)}) fusion(f32[1024,1152]{1,0:T(8,128)S(1)} %get-tuple-element.38, f32[1024]{0:T(1024)S(1)} %get-tuple-element.37, s32[1024]{0:T(1024)S(1)} %bitcast.24, s32[1152]{0:T(1024)S(1)} %iota_add_fusion), kind=kLoop, calls=%fused_computation.1 | loop fusion | flops 5896192 | bytes 4739584 | tf_op jit(solution)/shard_map/reduce_sum | solution.py:281
  104.2 0.6 concatenate.8.s_ref
  104.8 17.9 %shard_map.79 = f32[16,8,8,128]{3,2,1,0:T(8,128)} custom-call(f32[8,8,128]{2,1,0:T(8,128)} %concatenate.8.s_ref), custom_call_target="tpu_custom_call" | custom-call | tf_op jit(solution)/shard_map/pallas_call | solution.py:289
  122.7 1.6 %slice_reduce_fusion = (f32[128]{0:T(128)S(1)}, f32[128,1,128]{2,1,0:T(1,128)S(1)}, f32[128,1,128]{2,1,0:T(1,128)S(1)}) fusion(f32[128,8,128]{2,1,0:T(8,128)} %bitcast.17), kind=kLoop, calls=%fused_computation.7 | loop fusion | flops 16256 | bytes 328192 | tf_op jit(solution)/shard_map/reduce_sum | solution.py:303
  124.4 0.0 copy-done
  124.4 0.5 compare_select_fusion
  (5 shorter events, 0.1 us)
Async XLA Ops:
  102.4 21.9 %copy-start = (f32[128]{0:T(128)S(1)}, f32[128]{0:T(128)}, u32[]{:S(2)}) copy-start(f32[128]{0:T(128)} %param.14) | copy-start | bytes 1540

commit v4 on v3

--- a/solution.py
+++ b/solution.py
@@ -17,45 +17,6 @@
     for k in range(1, nt):
         pl.semaphore_signal(barrier, inc=1, device_id=(d, lax.rem(t + k, nt)), device_id_type=MESH)
     pl.semaphore_wait(barrier, nd - 1 + nt - 1)
-
-
-def _pre_kernel(nd, nt, ssq_ref, tgt_ref, q_out, t_out, q_buf, t_buf, q_send, q_recv, t_send, t_recv, local):
-    d = lax.axis_index("dp")
-    t = lax.axis_index("tensor")
-    _barrier(nd, nt, d, t)
-    own_q = pltpu.make_async_copy(ssq_ref, q_buf.at[t], local.at[0])
-    own_t = pltpu.make_async_copy(tgt_ref, t_buf.at[d], local.at[1])
-    own_q.start()
-    own_t.start()
-    sends = []
-    for k in range(1, nt):
-        c = pltpu.make_async_remote_copy(
-            src_ref=ssq_ref, dst_ref=q_buf.at[t], send_sem=q_send.at[k], recv_sem=q_recv.at[t],
-            device_id=(d, lax.rem(t + k, nt)), device_id_type=MESH)
-        c.start()
-        sends.append(c)
-    for k in range(1, nd):
-        c = pltpu.make_async_remote_copy(
-            src_ref=tgt_ref, dst_ref=t_buf.at[d], send_sem=t_send.at[k], recv_sem=t_recv.at[d],
-            device_id=(lax.rem(d + k, nd), t), device_id_type=MESH)
-        c.start()
-        sends.append(c)
-    for k in range(1, nt):
-        src = lax.rem(t + nt - k, nt)
-        pltpu.make_async_remote_copy(
-            src_ref=ssq_ref, dst_ref=q_buf.at[src], send_sem=q_send.at[k], recv_sem=q_recv.at[src],
-            device_id=(d, src), device_id_type=MESH).wait_recv()
-    for k in range(1, nd):
-        src = lax.rem(d + nd - k, nd)
-        pltpu.make_async_remote_copy(
-            src_ref=tgt_ref, dst_ref=t_buf.at[src], send_sem=t_send.at[k], recv_sem=t_recv.at[src],
-            device_id=(src, t), device_id_type=MESH).wait_recv()
-    for c in sends:
-        c.wait_send()
-    own_q.wait()
-    own_t.wait()
-    q_out[...] = q_buf[...]
-    t_out[...] = t_buf[...]
 
 
 def _stats_kernel(nd, nt, s_ref, out_ref, r1, r2, s1_send, s1_recv, s2_send, s2_recv, local):
@@ -106,7 +67,8 @@
     return lax.rem(v + RING, RING)
 
 
-def _gather_kernel(x_ref, out, ssem, rsem, psend, precv, lsem):
+def _gather_kernel(h_ref, g_ref, ssq_ref, tgt_ref, out, t_out, ssem, rsem, psend, precv, lsem,
+                   q_buf, t_buf, x_ref, q_send, q_recv, t_send, t_recv):
     d = lax.axis_index("dp")
     t = lax.axis_index("tensor")
     cc = lax.rem(t, 2)
@@ -144,7 +106,38 @@
         for delta in (1, -1):
             pl.semaphore_signal(barrier, inc=1, device_id=dev(moved(me, dim, delta)), device_id_type=MESH)
     pl.semaphore_signal(barrier, inc=1, device_id=partner, device_id_type=MESH)
-    pl.semaphore_wait(barrier, 7)
+    nd, nt = 2 * RING, RING * 2 * 2
+    for k in range(1, nd):
+        pl.semaphore_signal(barrier, inc=1, device_id=(lax.rem(d + k, nd), t), device_id_type=MESH)
+    for k in range(1, nt):
+        pl.semaphore_signal(barrier, inc=1, device_id=(d, lax.rem(t + k, nt)), device_id_type=MESH)
+    pl.semaphore_wait(barrier, 7 + nd - 1 + nt - 1)
+
+    small = []
+    for k in range(1, nt):
+        c = pltpu.make_async_remote_copy(
+            src_ref=ssq_ref, dst_ref=q_buf.at[t], send_sem=q_send.at[k], recv_sem=q_recv.at[t],
+            device_id=(d, lax.rem(t + k, nt)), device_id_type=MESH)
+        c.start()
+        small.append(c)
+    for k in range(1, nd):
+        c = pltpu.make_async_remote_copy(
+            src_ref=tgt_ref, dst_ref=t_buf.at[d], send_sem=t_send.at[k], recv_sem=t_recv.at[d],
+            device_id=(lax.rem(d + k, nd), t), device_id_type=MESH)
+        c.start()
+        small.append(c)
+    own_t = pltpu.make_async_copy(tgt_ref, t_buf.at[d], lsem.at[3])
+    own_t.start()
+    for k in range(1, nt):
+        src = lax.rem(t + nt - k, nt)
+        pltpu.make_async_remote_copy(
+            src_ref=ssq_ref, dst_ref=q_buf.at[src], send_sem=q_send.at[k], recv_sem=q_recv.at[src],
+            device_id=(d, src), device_id_type=MESH).wait_recv()
+    ssq = ssq_ref[...]
+    for k in range(1, nt):
+        ssq = ssq + q_buf[lax.rem(t + k, nt)]
+    scale = lax.rsqrt(jnp.transpose(ssq)[:, 0:1] / (nt * cols) + 1e-06)
+    x_ref[...] = (h_ref[...].astype(jnp.float32) * scale * g_ref[0:1, :]).astype(x_ref.dtype)
 
     fwd = []
 
@@ -209,6 +202,15 @@
             for di, delta in enumerate((1, -1)):
                 recv((r * 3 + k) * 4 + 2 + di, far, r, di, dev(moved(me, dim, -delta)))
                 to_partner(r, 3 + 4 * k + di, far, di)
+    for k in range(1, nd):
+        src = lax.rem(d + nd - k, nd)
+        pltpu.make_async_remote_copy(
+            src_ref=tgt_ref, dst_ref=t_buf.at[src], send_sem=t_send.at[k], recv_sem=t_recv.at[src],
+            device_id=(src, t), device_id_type=MESH).wait_recv()
+    for c in small:
+        c.wait_send()
+    own_t.wait()
+    t_out[...] = t_buf[...]
     for c in sends:
         c.wait_send()
     for j, n, r, half in fwd:
@@ -220,20 +222,27 @@
         c.wait_recv()
 
 
-def _gather(normed):
-    rows, cols = normed.shape
+def _gather(hidden, gain, ssq_in, tgt_in):
+    rows, cols = hidden.shape
+    nd, nt = 2 * RING, RING * 2 * 2
     return pl.pallas_call(
         _gather_kernel,
-        out_shape=jax.ShapeDtypeStruct((2 * RING * rows, RING * 2 * 2 * cols), normed.dtype),
-        in_specs=[pl.BlockSpec(memory_space=pltpu.VMEM)],
-        out_specs=pl.BlockSpec(memory_space=pl.ANY),
+        out_shape=(jax.ShapeDtypeStruct((nd * rows, nt * cols), jnp.bfloat16),
+                   jax.ShapeDtypeStruct((nd, 8, rows), jnp.int32)),
+        in_specs=[pl.BlockSpec(memory_space=pltpu.VMEM)] * 4,
+        out_specs=(pl.BlockSpec(memory_space=pl.ANY), pl.BlockSpec(memory_space=pltpu.VMEM)),
         scratch_shapes=[
             pltpu.SemaphoreType.DMA((36,)), pltpu.SemaphoreType.DMA((36,)),
             pltpu.SemaphoreType.DMA((39,)), pltpu.SemaphoreType.DMA((39,)),
-            pltpu.SemaphoreType.DMA((3,)),
+            pltpu.SemaphoreType.DMA((4,)),
+            pltpu.VMEM((nt, 8, rows), jnp.float32),
+            pltpu.VMEM((nd, 8, rows), jnp.int32),
+            pltpu.VMEM((rows, cols), jnp.bfloat16),
+            pltpu.SemaphoreType.DMA((nt,)), pltpu.SemaphoreType.DMA((nt,)),
+            pltpu.SemaphoreType.DMA((nd,)), pltpu.SemaphoreType.DMA((nd,)),
         ],
         compiler_params=pltpu.CompilerParams(collective_id=2, has_side_effects=True),
-    )(normed)
+    )(hidden, gain, ssq_in, tgt_in)
 
 
 def _vmem_call(kernel, out_shape, scratch, cid):
@@ -250,32 +259,15 @@
 
 def _body(nd, nt, hidden, norm_gain, head, targets, old_logprob, lengths):
     tok_rows = hidden.shape[0]
-    width = hidden.shape[1] * nt
-    lanes = 128
     values = hidden.astype(jnp.float32)
     part_sq = jnp.sum(values * values, axis=1)
 
     ssq_in = jnp.zeros((8, tok_rows), jnp.float32).at[0].set(part_sq)
     tgt_in = jnp.zeros((8, tok_rows), jnp.int32).at[0].set(targets)
-    pre = _vmem_call(
-        functools.partial(_pre_kernel, nd, nt),
-        (jax.ShapeDtypeStruct((nt, 8, tok_rows), jnp.float32),
-         jax.ShapeDtypeStruct((nd, 8, tok_rows), jnp.int32)),
-        [pltpu.VMEM((nt, 8, tok_rows), jnp.float32),
-         pltpu.VMEM((nd, 8, tok_rows), jnp.int32),
-         pltpu.SemaphoreType.DMA((nt,)), pltpu.SemaphoreType.DMA((nt,)),
-         pltpu.SemaphoreType.DMA((nd,)), pltpu.SemaphoreType.DMA((nd,)),
-         pltpu.SemaphoreType.DMA((2,))],
-        0,
-    )
-    q_all, t_all = pre(ssq_in, tgt_in)
-    sum_sq = jnp.sum(q_all[:, 0, :], axis=0)
+    gathered, t_all = _gather(hidden, jnp.broadcast_to(norm_gain[None, :], (8, norm_gain.shape[0])), ssq_in, tgt_in)
     target_all = t_all[:, 0, :].reshape(nd * tok_rows)
-
-    scaled = lax.rsqrt(sum_sq / width + 1e-06)
-    normed = (values * scaled[:, None] * norm_gain[None, :]).astype(jnp.bfloat16)
+    logits = jnp.dot(gathered, head, preferred_element_type=jnp.float32)
     vocab_cols = head.shape[1]
-    logits = jnp.dot(_gather(normed), head, preferred_element_type=jnp.float32)
     vocab_start = lax.axis_index(("dp", "tensor")) * vocab_cols
     block_top = jnp.max(logits, axis=1)
     block_total = jnp.sum(jnp.exp(logits - block_top[:, None]), axis=1)

time: 125 us -> 125 us (level)
  Pallas kernels: 86.5 us -> 83.7 us
  matrix products: 26.4 us -> 28.4 us
  local copies, waits for them, and re-layouts: 3.24 us -> 4.51 us
    pallas_call x2 -> x1, Pallas kernels: 68.6 us -> 66.2 us  [_gather(): pl.pallas_call(_gather_kernel, out_shape=(jax.ShapeDtypeStruct((nd * rows...]
    dot_general x1, matrix products: 26.4 us -> 28.4 us  [_body(): logits = jnp.dot(gathered, head, preferred_element_type=jnp.float32)]
    convert_element_type x1 -> x0, other arithmetic: 1.64 us -> none  [_body(): (values * scaled[:, None] * norm_gain[None, :]).astype(jnp.bfloat16)]
    reduce_sum x1, other arithmetic: 1.75 us -> 3.15 us  [_body(): block_total = jnp.sum(jnp.exp(logits - block_top[:, None]), axis=1)]
    broadcast_in_dim x0 -> x1, local copies, waits for them, and re-layouts: none -> 1.28 us  [_body(): jnp.broadcast_to(norm_gain[None, :], (8, norm_gain.shape[0]))]
where the time goes in v4:
time: 125 us; the launch traced here: 124 us
  Pallas kernels  83.7 us (67%)
  matrix products  28.4 us (23%)
  other arithmetic  6.36 us (5%)
  local copies, waits for them, and re-layouts  4.51 us (4%)
  between operations  1.32 us (1%)
    pallas_call x1, Pallas kernels, _gather(): pl.pallas_call(_gather_kernel, out_shape=(jax.ShapeDtypeStruct((nd * rows...  66.2 us
    dot_general x1, matrix products, _body(): logits = jnp.dot(gathered, head, preferred_element_type=jnp.float32)  28.4 us
    pallas_call x1, Pallas kernels, _body(): _vmem_call(functools.partial(_stats_kernel, nd, nt), jax.ShapeDtypeStruct...  17.5 us
    reduce_sum x1, other arithmetic, _body(): block_total = jnp.sum(jnp.exp(logits - block_top[:, None]), axis=1)  3.15 us

profile of v4, /device:TPU:1, one launch (start us, length us, event | category | flops | bytes accessed | tf_op | source)
XLA Modules:
  0.0 124.2 jit_solution(4344128986735242032)
XLA Ops:
  0.6 1.3 %broadcast_in_dim.5.g_ref = f32[8,512]{1,0:T(8,128)} broadcast(f32[512]{0:T(512)} %param.11), dimensions={1} | broadcast | bytes 18432 | tf_op jit(solution)/shard_map/broadcast_in_dim | solution.py:267
  1.9 1.0 multiply_reduce_fusion
  2.9 0.6 scatter.6.ssq_ref
  3.5 1.2 scatter.9.tgt_ref
  4.8 66.2 %shard_map.77 = (bf16[1024,8192]{1,0:T(8,128)(2,1)}, s32[8,8,128]{2,1,0:T(8,128)}) custom-call(bf16[128,512]{1,0:T(8,128)(2,1)} %h_ref.1, f32[8,512]{1,0:T(8,128)} %broadcast_in_dim.5.g_ref, f32[8,128]{1,0:T(8,128)} %scatter.6.ssq_ref, s32[8,128]{1,0:T(8,128)} %scatter.9.tgt_ref), custom_call_target="tpu_custom_call" | custom-call | tf_op jit(solution)/shard_map/pallas_call | solution.py:228
  71.0 28.4 %fusion = (f32[1024]{0:T(1024)S(1)}, f32[1024,1152]{1,0:T(8,128)}) fusion(bf16[1024,8192]{1,0:T(8,128)(2,1)} %get-tuple-element.28, bf16[8192,1152]{1,0:T(8,128)(2,1)} %param.12), kind=kOutput, calls=%fused_computation.10 | convolution fusion | flops 19328532480 | bytes 40374272 | tf_op jit(solution)/shard_map/dot_general | solution.py:269
  99.3 0.0 copy-start
  99.3 0.8 slice.40
  100.1 3.1 %exponential_reduce_fusion = (f32[1024]{0:T(1024)S(1)}, f32[1024]{0:T(1024)S(1)}) fusion(f32[1024,1152]{1,0:T(8,128)} %get-tuple-element.38, f32[1024]{0:T(1024)S(1)} %get-tuple-element.37, s32[1024]{0:T(1024)S(1)} %bitcast.24, s32[1152]{0:T(1024)S(1)} %iota_add_fusion), kind=kLoop, calls=%fused_computation.1 | loop fusion | flops 5896192 | bytes 4739584 | tf_op jit(solution)/shard_map/reduce_sum | solution.py:273
  103.3 0.6 concatenate.8.s_ref
  103.9 17.5 %shard_map.78 = f32[16,8,8,128]{3,2,1,0:T(8,128)} custom-call(f32[8,8,128]{2,1,0:T(8,128)} %concatenate.8.s_ref), custom_call_target="tpu_custom_call" | custom-call | tf_op jit(solution)/shard_map/pallas_call | solution.py:281
  121.4 1.6 %slice_reduce_fusion = (f32[128]{0:T(128)S(1)}, f32[128,1,128]{2,1,0:T(1,128)S(1)}, f32[128,1,128]{2,1,0:T(1,128)S(1)}) fusion(f32[128,8,128]{2,1,0:T(8,128)} %bitcast.17), kind=kLoop, calls=%fused_computation.3 | loop fusion | flops 16256 | bytes 328192 | tf_op jit(solution)/shard_map/reduce_sum | solution.py:295
  123.7 0.0 copy-done
  123.7 0.5 compare_select_fusion
  (4 shorter events, 0.1 us)
Async XLA Ops:
  99.3 24.4 %copy-start = (f32[128]{0:T(128)S(1)}, f32[128]{0:T(128)}, u32[]{:S(2)}) copy-start(f32[128]{0:T(128)} %param.14) | copy-start | bytes 1540

commit v5 on v4

--- a/solution.py
+++ b/solution.py
@@ -262,9 +262,9 @@
     values = hidden.astype(jnp.float32)
     part_sq = jnp.sum(values * values, axis=1)
 
-    ssq_in = jnp.zeros((8, tok_rows), jnp.float32).at[0].set(part_sq)
-    tgt_in = jnp.zeros((8, tok_rows), jnp.int32).at[0].set(targets)
-    gathered, t_all = _gather(hidden, jnp.broadcast_to(norm_gain[None, :], (8, norm_gain.shape[0])), ssq_in, tgt_in)
+    ssq_in = jnp.broadcast_to(part_sq[None, :], (8, tok_rows))
+    tgt_in = jnp.broadcast_to(targets[None, :], (8, tok_rows))
+    gathered, t_all = _gather(hidden, norm_gain[None, :], ssq_in, tgt_in)
     target_all = t_all[:, 0, :].reshape(nd * tok_rows)
     logits = jnp.dot(gathered, head, preferred_element_type=jnp.float32)
     vocab_cols = head.shape[1]
@@ -275,9 +275,8 @@
     hits = column[None, :] == target_all[:, None]
     block_pick = jnp.sum(jnp.where(hits, logits, jnp.float32(0.0)), axis=1)
 
-    stacked = jnp.stack([block_top, block_total, block_pick], axis=0).reshape(3, nd, tok_rows)
-    stacked = jnp.transpose(stacked, (1, 0, 2))
-    s_in = jnp.concatenate([stacked, jnp.zeros((nd, 5, tok_rows), jnp.float32)], axis=1)
+    stacked = jnp.stack([block_top, block_total, block_pick] + [block_top] * 5, axis=0).reshape(8, nd, tok_rows)
+    s_in = jnp.transpose(stacked, (1, 0, 2))
     stats = _vmem_call(
         functools.partial(_stats_kernel, nd, nt),
         jax.ShapeDtypeStruct((nt, nd, 8, tok_rows), jnp.float32),

time: 125 us -> 123 us (0.984)
    scatter x2 -> x0, local copies, waits for them, and re-layouts: 1.85 us -> none  [the longest x1 1.24 us: _body(): tgt_in = jnp.zeros((8, tok_rows), jnp.int32).at[0].set(targets)]
where the time goes in v5:
time: 123 us
  Pallas kernels  83.6 us (68%)
  matrix products  28.4 us (23%)
  other arithmetic  6.42 us (5%)
  local copies, waits for them, and re-layouts  3.28 us (3%)
  between operations  1.31 us (1%)
    pallas_call x1, Pallas kernels, _gather(): pl.pallas_call(_gather_kernel, out_shape=(jax.ShapeDtypeStruct((nd * rows...  66.2 us
    dot_general x1, matrix products, _body(): logits = jnp.dot(gathered, head, preferred_element_type=jnp.float32)  28.4 us
    pallas_call x1, Pallas kernels, _body(): _vmem_call(functools.partial(_stats_kernel, nd, nt), jax.ShapeDtypeStruct...  17.5 us
    reduce_sum x1, other arithmetic, _body(): block_pick = jnp.sum(jnp.where(hits, logits, jnp.float32(0.0)), axis=1)  3.23 us

profile of v5, /device:TPU:1, one launch (start us, length us, event | category | flops | bytes accessed | tf_op | source)
XLA Modules:
  0.0 123.0 jit_solution(1716608579670537463)
XLA Ops:
  0.6 1.0 multiply_reduce_fusion
  1.6 0.6 broadcast_in_dim.10.ssq_ref
  2.2 1.2 %broadcast_in_dim.11.tgt_ref = s32[8,128]{1,0:T(8,128)} broadcast(s32[128]{0:T(128)} %param.9), dimensions={1} | broadcast | bytes 4608 | tf_op jit(solution)/shard_map/broadcast_in_dim | solution.py:266
  3.5 66.2 %shard_map.77 = (bf16[1024,8192]{1,0:T(8,128)(2,1)}, s32[8,8,128]{2,1,0:T(8,128)}) custom-call(bf16[128,512]{1,0:T(8,128)(2,1)} %h_ref.1, f32[1,512]{1,0:T(1,128)} %bitcast.29, f32[8,128]{1,0:T(8,128)} %broadcast_in_dim.10.ssq_ref, s32[8,128]{1,0:T(8,128)} %broadcast_in_dim.11.tgt_ref), custom_call_target="tpu_custom_call" | custom-call | tf_op jit(solution)/shard_map/pallas_call | solution.py:228
  69.7 28.4 %fusion = (f32[1024]{0:T(1024)S(1)}, f32[1024,1152]{1,0:T(8,128)}) fusion(bf16[1024,8192]{1,0:T(8,128)(2,1)} %get-tuple-element.4, bf16[8192,1152]{1,0:T(8,128)(2,1)} %param.8), kind=kOutput, calls=%fused_computation.9 | convolution fusion | flops 19328532480 | bytes 40374272 | tf_op jit(solution)/shard_map/dot_general | solution.py:269
  98.0 0.0 copy-start
  98.0 0.8 slice.12
  98.8 3.2 %select_reduce_fusion = (f32[1024]{0:T(1024)S(1)}, f32[1024]{0:T(1024)S(1)}) fusion(f32[1024,1152]{1,0:T(8,128)} %get-tuple-element.14, s32[1152]{0:T(1024)S(1)} %iota_add_fusion, s32[1024]{0:T(1024)S(1)} %bitcast.28, f32[1024]{0:T(1024)S(1)} %get-tuple-element.13), kind=kLoop, calls=%fused_computation | loop fusion | flops 5896192 | bytes 4739584 | tf_op jit(solution)/shard_map/reduce_sum | solution.py:276
  102.0 0.7 stack.20
  102.7 17.5 %shard_map.78 = f32[16,8,8,128]{3,2,1,0:T(8,128)} custom-call(f32[8,8,128]{2,1,0:T(8,128)} %bitcast.25), custom_call_target="tpu_custom_call" | custom-call | tf_op jit(solution)/shard_map/pallas_call | solution.py:280
  120.2 1.6 %slice_reduce_fusion = (f32[128]{0:T(128)S(1)}, f32[128,1,128]{2,1,0:T(1,128)S(1)}, f32[128,1,128]{2,1,0:T(1,128)S(1)}) fusion(f32[128,8,128]{2,1,0:T(8,128)} %bitcast.15), kind=kLoop, calls=%fused_computation.3 | loop fusion | flops 16256 | bytes 328192 | tf_op jit(solution)/shard_map/reduce_sum | solution.py:294
  122.5 0.0 copy-done
  122.5 0.5 compare_select_fusion
  (3 shorter events, 0.1 us)
Async XLA Ops:
  98.0 24.4 %copy-start = (f32[128]{0:T(128)S(1)}, f32[128]{0:T(128)}, u32[]{:S(2)}) copy-start(f32[128]{0:T(128)} %param.10) | copy-start | bytes 1540

commit v6 on v5

--- a/solution.py
+++ b/solution.py
@@ -182,26 +182,33 @@
             src_ref=v, dst_ref=v, send_sem=ssem.at[group], recv_sem=rsem.at[group],
             device_id=dst_dev, device_id_type=MESH))
 
+    later = []
     for k in range(3):
         for r in range(3):
             dim = ORDERS[r][k]
             for di, delta in enumerate((1, -1)):
                 send((r * 3 + k) * 4 + di, slab(r, k, me), r, None, dev(moved(me, dim, delta)))
+        for args in later:
+            to_partner(*args)
+        later = []
         for r in range(3):
             dim = ORDERS[r][k]
             for di, delta in enumerate((1, -1)):
                 near = slab(r, k, moved(me, dim, -delta))
                 recv((r * 3 + k) * 4 + di, near, r, None, dev(moved(me, dim, -delta)))
-                to_partner(r, 1 + 4 * k + di, near, None)
             for di, delta in enumerate((1, -1)):
                 near = slab(r, k, moved(me, dim, -delta))
                 send((r * 3 + k) * 4 + 2 + di, near, r, di, dev(moved(me, dim, delta)))
+            for di, delta in enumerate((1, -1)):
+                to_partner(r, 1 + 4 * k + di, slab(r, k, moved(me, dim, -delta)), None)
         for r in range(3):
             dim = ORDERS[r][k]
             far = slab(r, k, moved(me, dim, 2))
             for di, delta in enumerate((1, -1)):
                 recv((r * 3 + k) * 4 + 2 + di, far, r, di, dev(moved(me, dim, -delta)))
-                to_partner(r, 3 + 4 * k + di, far, di)
+                later.append((r, 3 + 4 * k + di, far, di))
+    for args in later:
+        to_partner(*args)
     for k in range(1, nd):
         src = lax.rem(d + nd - k, nd)
         pltpu.make_async_remote_copy(

time: 123 us -> 123 us (level)
  no operation moved by 1% of the time
where the time goes in v6:
time: 123 us
  Pallas kernels  83.5 us (68%)
  matrix products  28.4 us (23%)
  other arithmetic  6.42 us (5%)
  local copies, waits for them, and re-layouts  3.28 us (3%)
  between operations  1.31 us (1%)
    pallas_call x1, Pallas kernels, _gather(): pl.pallas_call(_gather_kernel, out_shape=(jax.ShapeDtypeStruct((nd * rows...  66.8 us
    dot_general x1, matrix products, _body(): logits = jnp.dot(gathered, head, preferred_element_type=jnp.float32)  28.4 us
    pallas_call x1, Pallas kernels, _body(): _vmem_call(functools.partial(_stats_kernel, nd, nt), jax.ShapeDtypeStruct...  16.7 us
    reduce_sum x1, other arithmetic, _body(): block_pick = jnp.sum(jnp.where(hits, logits, jnp.float32(0.0)), axis=1)  3.23 us

profile of v6, /device:TPU:1, one launch (start us, length us, event | category | flops | bytes accessed | tf_op | source)
XLA Modules:
  0.0 122.9 jit_solution(9835389798748681193)
XLA Ops:
  0.6 1.0 multiply_reduce_fusion
  1.6 0.6 broadcast_in_dim.10.ssq_ref
  2.2 1.2 %broadcast_in_dim.11.tgt_ref = s32[8,128]{1,0:T(8,128)} broadcast(s32[128]{0:T(128)} %param.9), dimensions={1} | broadcast | bytes 4608 | tf_op jit(solution)/shard_map/broadcast_in_dim | solution.py:273
  3.5 66.8 %shard_map.77 = (bf16[1024,8192]{1,0:T(8,128)(2,1)}, s32[8,8,128]{2,1,0:T(8,128)}) custom-call(bf16[128,512]{1,0:T(8,128)(2,1)} %h_ref.1, f32[1,512]{1,0:T(1,128)} %bitcast.29, f32[8,128]{1,0:T(8,128)} %broadcast_in_dim.10.ssq_ref, s32[8,128]{1,0:T(8,128)} %broadcast_in_dim.11.tgt_ref), custom_call_target="tpu_custom_call" | custom-call | tf_op jit(solution)/shard_map/pallas_call | solution.py:235
  70.3 28.4 %fusion = (f32[1024]{0:T(1024)S(1)}, f32[1024,1152]{1,0:T(8,128)}) fusion(bf16[1024,8192]{1,0:T(8,128)(2,1)} %get-tuple-element.4, bf16[8192,1152]{1,0:T(8,128)(2,1)} %param.8), kind=kOutput, calls=%fused_computation.9 | convolution fusion | flops 19328532480 | bytes 40374272 | tf_op jit(solution)/shard_map/dot_general | solution.py:276
  98.6 0.0 copy-start
  98.6 0.8 slice.12
  99.4 3.2 %select_reduce_fusion = (f32[1024]{0:T(1024)S(1)}, f32[1024]{0:T(1024)S(1)}) fusion(f32[1024,1152]{1,0:T(8,128)} %get-tuple-element.14, s32[1152]{0:T(1024)S(1)} %iota_add_fusion, s32[1024]{0:T(1024)S(1)} %bitcast.28, f32[1024]{0:T(1024)S(1)} %get-tuple-element.13), kind=kLoop, calls=%fused_computation | loop fusion | flops 5896192 | bytes 4739584 | tf_op jit(solution)/shard_map/reduce_sum | solution.py:283
  102.6 0.7 stack.20
  103.3 16.7 %shard_map.78 = f32[16,8,8,128]{3,2,1,0:T(8,128)} custom-call(f32[8,8,128]{2,1,0:T(8,128)} %bitcast.25), custom_call_target="tpu_custom_call" | custom-call | tf_op jit(solution)/shard_map/pallas_call | solution.py:287
  120.1 1.6 %slice_reduce_fusion = (f32[128]{0:T(128)S(1)}, f32[128,1,128]{2,1,0:T(1,128)S(1)}, f32[128,1,128]{2,1,0:T(1,128)S(1)}) fusion(f32[128,8,128]{2,1,0:T(8,128)} %bitcast.15), kind=kLoop, calls=%fused_computation.3 | loop fusion | flops 16256 | bytes 328192 | tf_op jit(solution)/shard_map/reduce_sum | solution.py:301
  122.4 0.0 copy-done
  122.4 0.5 compare_select_fusion
  (3 shorter events, 0.1 us)
Async XLA Ops:
  98.6 23.7 %copy-start = (f32[128]{0:T(128)S(1)}, f32[128]{0:T(128)}, u32[]{:S(2)}) copy-start(f32[128]{0:T(128)} %param.10) | copy-start | bytes 1540

commit v7 on v6

--- a/solution.py
+++ b/solution.py
@@ -273,14 +273,21 @@
     tgt_in = jnp.broadcast_to(targets[None, :], (8, tok_rows))
     gathered, t_all = _gather(hidden, norm_gain[None, :], ssq_in, tgt_in)
     target_all = t_all[:, 0, :].reshape(nd * tok_rows)
-    logits = jnp.dot(gathered, head, preferred_element_type=jnp.float32)
     vocab_cols = head.shape[1]
     vocab_start = lax.axis_index(("dp", "tensor")) * vocab_cols
-    block_top = jnp.max(logits, axis=1)
-    block_total = jnp.sum(jnp.exp(logits - block_top[:, None]), axis=1)
     column = vocab_start + jnp.arange(vocab_cols, dtype=jnp.int32)
-    hits = column[None, :] == target_all[:, None]
-    block_pick = jnp.sum(jnp.where(hits, logits, jnp.float32(0.0)), axis=1)
+
+    def block_stats(rows, tgt):
+        logits = jnp.dot(rows, head, preferred_element_type=jnp.float32)
+        top = jnp.max(logits, axis=1)
+        total = jnp.sum(jnp.exp(logits - top[:, None]), axis=1)
+        hits = column[None, :] == tgt[:, None]
+        return top, total, jnp.sum(jnp.where(hits, logits, jnp.float32(0.0)), axis=1)
+
+    split = gathered.shape[0] // 2
+    first = block_stats(gathered[:split], target_all[:split])
+    second = block_stats(gathered[split:], target_all[split:])
+    block_top, block_total, block_pick = (jnp.concatenate([a, b]) for a, b in zip(first, second))
 
     stacked = jnp.stack([block_top, block_total, block_pick] + [block_top] * 5, axis=0).reshape(8, nd, tok_rows)
     s_in = jnp.transpose(stacked, (1, 0, 2))

time: 123 us -> 126 us (1.024)
  matrix products: 28.4 us -> 32.8 us
  other arithmetic: 6.42 us -> 4.84 us
    dot_general x1 -> x2, matrix products: 28.4 us -> 32.8 us  [block_stats(): logits = jnp.dot(rows, head, preferred_element_type=jnp.float32)]
    reduce_sum x1, other arithmetic: 3.23 us -> 1.63 us  [block_stats(): jnp.sum(jnp.where(hits, logits, jnp.float32(0.0)), axis=1)]
where the time goes in v7:
time: 126 us
  Pallas kernels  83.5 us (66%)
  matrix products  32.8 us (26%)
  other arithmetic  4.84 us (4%)
  local copies, waits for them, and re-layouts  3.24 us (3%)
  between operations  1.34 us (1%)
    pallas_call x1, Pallas kernels, _gather(): pl.pallas_call(_gather_kernel, out_shape=(jax.ShapeDtypeStruct((nd * rows...  66.8 us
    dot_general x2, matrix products, block_stats(): logits = jnp.dot(rows, head, preferred_element_type=jnp.float32)  32.8 us
    pallas_call x1, Pallas kernels, _body(): _vmem_call(functools.partial(_stats_kernel, nd, nt), jax.ShapeDtypeStruct...  16.8 us

profile of v7, /device:TPU:1, one launch (start us, length us, event | category | flops | bytes accessed | tf_op | source)
XLA Modules:
  0.0 125.8 jit_solution(7652570040776267602)
XLA Ops:
  1.3 1.0 multiply_reduce_fusion
  2.3 0.6 broadcast_in_dim.11.ssq_ref
  2.9 1.2 broadcast_in_dim.12.tgt_ref
  4.1 66.8 %shard_map.77 = (bf16[1024,8192]{1,0:T(8,128)(2,1)}, s32[8,8,128]{2,1,0:T(8,128)}) custom-call(bf16[128,512]{1,0:T(8,128)(2,1)} %h_ref.1, f32[1,512]{1,0:T(1,128)} %bitcast.31, f32[8,128]{1,0:T(8,128)} %broadcast_in_dim.11.ssq_ref, s32[8,128]{1,0:T(8,128)} %broadcast_in_dim.12.tgt_ref), custom_call_target="tpu_custom_call" | custom-call | tf_op jit(solution)/shard_map/pallas_call | solution.py:235
  70.9 0.7 fusion.4
  71.7 16.3 %fusion.5 = (f32[512]{0:T(512)S(1)}, f32[512,1152]{1,0:T(8,128)S(1)}) fusion(bf16[8192,1152]{1,0:T(8,128)(2,1)} %param.8, bf16[1024,8192]{1,0:T(8,128)(2,1)} %get-tuple-element.4), kind=kOutput, calls=%fused_computation.19 | convolution fusion | flops 9664266240 | bytes 29624320 | tf_op jit(solution)/shard_map/dot_general | solution.py:281
  88.0 16.5 %fusion.6 = (f32[512]{0:T(512)S(1)}, f32[512,1152]{1,0:T(8,128)S(1)}) fusion(bf16[8192,1152]{1,0:T(8,128)(2,1)} %param.8, bf16[1024,8192]{1,0:T(8,128)(2,1)} %get-tuple-element.4), kind=kOutput, calls=%fused_computation.20 | convolution fusion | flops 9664266240 | bytes 29624320 | tf_op jit(solution)/shard_map/dot_general | solution.py:281
  104.5 0.0 copy-start
  104.5 1.6 %select_reduce_fusion.1 = (f32[512]{0:T(512)S(1)}, f32[512]{0:T(512)S(1)}, f32[512]{0:T(512)S(1)}, f32[512]{0:T(512)S(1)}) fusion(f32[512,1152]{1,0:T(8,128)S(1)} %get-tuple-element.22, s32[1152]{0:T(1024)S(1)} %iota_add_fusion, s32[512]{0:T(512)S(1)} %bitcast.30, f32[512]{0:T(512)S(1)} %get-tuple-element.21, f32[512,1152]{1,0:T(8,128)S(1)} %get-tuple-element.20, ...), kind=kLoop, calls=%fused_computation.5 | loop fusion | flops 5896192 | bytes 4739584 | tf_op jit(solution)/shard_map/reduce_sum | solution.py:285
  106.1 0.7 stack.20
  106.8 16.8 %shard_map.78 = f32[16,8,8,128]{3,2,1,0:T(8,128)} custom-call(f32[8,8,128]{2,1,0:T(8,128)} %bitcast.26), custom_call_target="tpu_custom_call" | custom-call | tf_op jit(solution)/shard_map/pallas_call | solution.py:294
  123.6 1.6 %slice_reduce_fusion = (f32[128]{0:T(128)S(1)}, f32[128,1,128]{2,1,0:T(1,128)S(1)}, f32[128,1,128]{2,1,0:T(1,128)S(1)}) fusion(f32[128,8,128]{2,1,0:T(8,128)} %bitcast.16), kind=kLoop, calls=%fused_computation.9 | loop fusion | flops 16256 | bytes 328192 | tf_op jit(solution)/shard_map/reduce_sum | solution.py:308
  125.2 0.0 copy-done
  125.2 0.5 compare_select_fusion
  (5 shorter events, 0.1 us)
Async XLA Ops:
  104.5 20.8 %copy-start = (f32[128]{0:T(128)S(1)}, f32[128]{0:T(128)}, u32[]{:S(2)}) copy-start(f32[128]{0:T(128)} %param.10) | copy-start | bytes 1540

commit v8 on v6

--- a/solution.py
+++ b/solution.py
@@ -10,51 +10,29 @@
 MESH = pl.DeviceIdType.MESH
 
 
-def _barrier(nd, nt, d, t):
-    barrier = pltpu.get_barrier_semaphore()
-    for k in range(1, nd):
-        pl.semaphore_signal(barrier, inc=1, device_id=(lax.rem(d + k, nd), t), device_id_type=MESH)
-    for k in range(1, nt):
-        pl.semaphore_signal(barrier, inc=1, device_id=(d, lax.rem(t + k, nt)), device_id_type=MESH)
-    pl.semaphore_wait(barrier, nd - 1 + nt - 1)
-
-
-def _stats_kernel(nd, nt, s_ref, out_ref, r1, r2, s1_send, s1_recv, s2_send, s2_recv, local):
+def _stats_kernel(nd, nt, s_ref, out_ref, r2, send_sem, recv_sem, local):
+    n = nd * nt
     d = lax.axis_index("dp")
     t = lax.axis_index("tensor")
-    _barrier(nd, nt, d, t)
-    own1 = pltpu.make_async_copy(s_ref.at[d], r1.at[d], local.at[0])
-    own1.start()
-    sends = []
-    for k in range(1, nd):
-        peer = lax.rem(d + k, nd)
-        c = pltpu.make_async_remote_copy(
-            src_ref=s_ref.at[peer], dst_ref=r1.at[d], send_sem=s1_send.at[k], recv_sem=s1_recv.at[d],
-            device_id=(peer, t), device_id_type=MESH)
-        c.start()
-        sends.append(c)
-    for k in range(1, nd):
-        src = lax.rem(d + nd - k, nd)
+    me = d * nt + t
+    barrier = pltpu.get_barrier_semaphore()
+    for k in range(1, n):
+        peer = lax.rem(me + k, n)
+        pl.semaphore_signal(barrier, inc=1, device_id=(peer // nt, lax.rem(peer, nt)), device_id_type=MESH)
+    pl.semaphore_wait(barrier, n - 1)
+    own = pltpu.make_async_copy(s_ref.at[d], r2.at[me], local.at[0])
+    own.start()
+    for k in range(1, n):
+        peer = lax.rem(me + k, n)
         pltpu.make_async_remote_copy(
-            src_ref=s_ref.at[0], dst_ref=r1.at[src], send_sem=s1_send.at[k], recv_sem=s1_recv.at[src],
-            device_id=(src, t), device_id_type=MESH).wait_recv()
-    own1.wait()
-    own2 = pltpu.make_async_copy(r1, r2.at[t], local.at[1])
-    own2.start()
-    for k in range(1, nt):
-        c = pltpu.make_async_remote_copy(
-            src_ref=r1, dst_ref=r2.at[t], send_sem=s2_send.at[k], recv_sem=s2_recv.at[t],
-            device_id=(d, lax.rem(t + k, nt)), device_id_type=MESH)
-        c.start()
-        sends.append(c)
-    for k in range(1, nt):
-        src = lax.rem(t + nt - k, nt)
-        pltpu.make_async_remote_copy(
-            src_ref=r1, dst_ref=r2.at[src], send_sem=s2_send.at[k], recv_sem=s2_recv.at[src],
-            device_id=(d, src), device_id_type=MESH).wait_recv()
-    for c in sends:
-        c.wait_send()
-    own2.wait()
+            src_ref=s_ref.at[peer // nt], dst_ref=r2.at[me], send_sem=send_sem, recv_sem=recv_sem,
+            device_id=(peer // nt, lax.rem(peer, nt)), device_id_type=MESH).start()
+    whole = pltpu.make_async_remote_copy(
+        src_ref=r2.at[pl.ds(0, n - 1)], dst_ref=r2.at[pl.ds(0, n - 1)], send_sem=send_sem, recv_sem=recv_sem,
+        device_id=(d, t), device_id_type=MESH)
+    whole.wait_recv()
+    whole.wait_send()
+    own.wait()
     out_ref[...] = r2[...]
 
 
@@ -286,12 +264,10 @@
     s_in = jnp.transpose(stacked, (1, 0, 2))
     stats = _vmem_call(
         functools.partial(_stats_kernel, nd, nt),
-        jax.ShapeDtypeStruct((nt, nd, 8, tok_rows), jnp.float32),
-        [pltpu.VMEM((nd, 8, tok_rows), jnp.float32),
-         pltpu.VMEM((nt, nd, 8, tok_rows), jnp.float32),
-         pltpu.SemaphoreType.DMA((nd,)), pltpu.SemaphoreType.DMA((nd,)),
-         pltpu.SemaphoreType.DMA((nt,)), pltpu.SemaphoreType.DMA((nt,)),
-         pltpu.SemaphoreType.DMA((2,))],
+        jax.ShapeDtypeStruct((nt * nd, 8, tok_rows), jnp.float32),
+        [pltpu.VMEM((nt * nd, 8, tok_rows), jnp.float32),
+         pltpu.SemaphoreType.DMA, pltpu.SemaphoreType.DMA,
+         pltpu.SemaphoreType.DMA((1,))],
         1,
     )(s_in)
     pieces = stats.reshape(nt * nd, 8, tok_rows)

time: 123 us -> 123 us (level)
  no operation moved by 1% of the time
where the time goes in v8:
time: 123 us
  Pallas kernels  83.4 us (68%)
  matrix products  28.4 us (23%)
  other arithmetic  6.6 us (5%)
  local copies, waits for them, and re-layouts  3.28 us (3%)
  between operations  1.32 us (1%)
    pallas_call x1, Pallas kernels, _gather(): pl.pallas_call(_gather_kernel, out_shape=(jax.ShapeDtypeStruct((nd * rows...  66.8 us
    dot_general x1, matrix products, _body(): logits = jnp.dot(gathered, head, preferred_element_type=jnp.float32)  28.4 us
    pallas_call x1, Pallas kernels, _body(): _vmem_call(functools.partial(_stats_kernel, nd, nt), jax.ShapeDtypeStruct...  16.6 us
    reduce_sum x1, other arithmetic, _body(): block_pick = jnp.sum(jnp.where(hits, logits, jnp.float32(0.0)), axis=1)  3.4 us

profile of v8, /device:TPU:1, one launch (start us, length us, event | category | flops | bytes accessed | tf_op | source)
XLA Modules:
  0.0 123.0 jit_solution(9350254967780693312)
XLA Ops:
  0.6 1.0 multiply_reduce_fusion
  1.6 0.6 broadcast_in_dim.10.ssq_ref
  2.2 1.2 %broadcast_in_dim.11.tgt_ref = s32[8,128]{1,0:T(8,128)} broadcast(s32[128]{0:T(128)} %param.9), dimensions={1} | broadcast | bytes 4608 | tf_op jit(solution)/shard_map/broadcast_in_dim | solution.py:251
  3.5 66.8 %shard_map.77 = (bf16[1024,8192]{1,0:T(8,128)(2,1)}, s32[8,8,128]{2,1,0:T(8,128)}) custom-call(bf16[128,512]{1,0:T(8,128)(2,1)} %h_ref.1, f32[1,512]{1,0:T(1,128)} %bitcast.27, f32[8,128]{1,0:T(8,128)} %broadcast_in_dim.10.ssq_ref, s32[8,128]{1,0:T(8,128)} %broadcast_in_dim.11.tgt_ref), custom_call_target="tpu_custom_call" | custom-call | tf_op jit(solution)/shard_map/pallas_call | solution.py:213
  70.3 28.4 %fusion = (f32[1024]{0:T(1024)S(1)}, f32[1024,1152]{1,0:T(8,128)}) fusion(bf16[1024,8192]{1,0:T(8,128)(2,1)} %get-tuple-element.4, bf16[8192,1152]{1,0:T(8,128)(2,1)} %param.8), kind=kOutput, calls=%fused_computation.9 | convolution fusion | flops 19328532480 | bytes 40374272 | tf_op jit(solution)/shard_map/dot_general | solution.py:254
  98.6 0.0 copy-start
  98.6 0.8 slice.12
  99.4 3.4 %select_reduce_fusion = (f32[1024]{0:T(1024)S(1)}, f32[1024]{0:T(1024)S(1)}) fusion(f32[1024,1152]{1,0:T(8,128)} %get-tuple-element.14, s32[1152]{0:T(1024)S(1)} %iota_add_fusion, s32[1024]{0:T(1024)S(1)} %bitcast.26, f32[1024]{0:T(1024)S(1)} %get-tuple-element.13), kind=kLoop, calls=%fused_computation | loop fusion | flops 5896192 | bytes 4739584 | tf_op jit(solution)/shard_map/reduce_sum | solution.py:261
  102.8 0.7 stack.20
  103.5 16.6 %shard_map.78 = f32[128,8,128]{2,1,0:T(8,128)} custom-call(f32[8,8,128]{2,1,0:T(8,128)} %bitcast.23), custom_call_target="tpu_custom_call" | custom-call | tf_op jit(solution)/shard_map/pallas_call | solution.py:265
  120.1 1.6 %slice_reduce_fusion = (f32[128]{0:T(128)S(1)}, f32[128,1,128]{2,1,0:T(1,128)S(1)}, f32[128,1,128]{2,1,0:T(1,128)S(1)}) fusion(f32[128,8,128]{2,1,0:T(8,128)} %shard_map.78), kind=kLoop, calls=%fused_computation.4 | loop fusion | flops 16256 | bytes 328192 | tf_op jit(solution)/shard_map/reduce_sum | solution.py:277
  122.4 0.0 copy-done
  122.4 0.5 compare_select_fusion
  (3 shorter events, 0.1 us)
Async XLA Ops:
  98.6 23.8 %copy-start = (f32[128]{0:T(128)S(1)}, f32[128]{0:T(128)}, u32[]{:S(2)}) copy-start(f32[128]{0:T(128)} %param.10) | copy-start | bytes 1540
